TPU v7x, 32 devices: a whole 2x2x4 slice. The times are simulated.
32 devices in a mesh: row: 4 (over y, x), col: 8 (over z, core).
Axes of the slice: x: 2, y: 2, z: 4, core: 2. Of those that a mesh axis runs over, the one named last changes fastest.
Arguments:
- noise: float32 [2048, 3072], P('row', 'col'), may hold values from -30 to 30
- images: float32 [6144, 3072], P('col', 'row'), may hold values from -6 to 6
- time_index: int32 [2048], P('row'), may hold values from 0 to 999
- w_in: float32 [3072, 3072], P(None, 'col'), may hold values from -0.109375 to 0.109375
- time_gain: float32 [3072], P('col'), may hold values from -5 to 5
- w_out: float32 [3072, 3072], P('col'), may hold values from -0.109375 to 0.109375
Outputs:
- targets: float32 [2048, 3072], P('row', 'col')
- row_pot: float32 [2048], P('row')
- col_pot: float32 [6144], P('col')
- grad_in: float32 [3072, 3072], P('row', 'col')
- grad_time: float32 [3072], P('col')
- grad_out: float32 [3072, 3072], P('col', 'row')
- mse: float32 [], replicated
All inputs are finite; a program needn't handle non-finite values.
Results may differ from a plain program's by a relative error of at most 0.0003.
Values sent between devices are 32-bit elements; how exact they have to be, the bound alone decides.
A program may use at most 128 MiB of HBM per device.

v0:
```python
import jax
import jax.numpy as jnp
from jax import lax
from jax.sharding import PartitionSpec as P

ITERS = 2
TIMES = 1000


EPSILON = 0.01


def merged(array, axis, combine):
    everything = jax.tree.map(lambda part: lax.all_gather(part, axis), array)
    first = jax.tree.map(lambda part: part[0], everything)

    def hop(k, so_far):
        return combine(so_far, jax.tree.map(lambda part: part[k], everything))

    return lax.fori_loop(1, lax.axis_size(axis), hop, first)


def joined(left_pair, right_pair):
    peak = jnp.maximum(left_pair[0], right_pair[0])
    total = left_pair[1] * jnp.exp(left_pair[0] - peak) + right_pair[1] * jnp.exp(
        right_pair[0] - peak
    )
    return (peak, total)


def over_images(logits):
    local_peak = jnp.max(logits, axis=1)
    local_total = jnp.sum(jnp.exp(logits - local_peak[:, None]), axis=1)
    peak, total = merged((local_peak, local_total), "col", joined)
    return (peak, total)


def over_noise(logits):
    local_peak = jnp.max(logits, axis=0)
    local_total = jnp.sum(jnp.exp(logits - local_peak[None, :]), axis=0)
    peak, total = merged((local_peak, local_total), "row", joined)
    return (peak, total)


def body(noise, images, time_index, w_in, time_gain, w_out):
    highest = lax.Precision.HIGHEST
    full_noise = lax.all_gather(noise, "col", axis=1, tiled=True)
    full_images = lax.all_gather(images, "row", axis=1, tiled=True)
    width = full_noise.shape[1]
    noise_count = full_noise.shape[0] * lax.axis_size("row")
    image_count = full_images.shape[0] * lax.axis_size("col")
    noise_norms = jnp.sum(full_noise * full_noise, axis=1)
    image_norms = jnp.sum(full_images * full_images, axis=1)
    cross = lax.dot_general(
        full_noise,
        full_images,
        (((1,), (1,)), ((), ())),
        precision=highest,
        preferred_element_type=jnp.float32,
    )
    scaled = (noise_norms[:, None] + image_norms[None, :] - 2.0 * cross) / (width * EPSILON)
    col_pot = jnp.zeros((full_images.shape[0],), jnp.float32)
    row_pot = jnp.zeros((full_noise.shape[0],), jnp.float32)
    for iteration in range(ITERS):
        peak, total = over_images(col_pot[None, :] - scaled)
        row_pot = jnp.log(jnp.float32(image_count)) - (jnp.log(total) + peak)
        peak, total = over_noise(row_pot[:, None] - scaled)
        col_pot = jnp.log(jnp.float32(noise_count)) - (jnp.log(total) + peak)
    logits = col_pot[None, :] - scaled
    peak, total = over_images(logits)
    weights = jnp.exp(logits - (jnp.log(total) + peak)[:, None])
    partial_value = jnp.dot(
        weights, full_images, precision=highest, preferred_element_type=jnp.float32
    )
    slice_width = noise.shape[1]
    slice_start = lax.axis_index("col") * slice_width
    whole_targets = lax.psum(partial_value, "col")
    targets = lax.dynamic_slice_in_dim(whole_targets, slice_start, slice_width, 1)
    fraction = (time_index.astype(jnp.float32) + 0.5) / TIMES
    mixed = (1.0 - fraction)[:, None] * full_noise + fraction[:, None] * whole_targets
    velocity = whole_targets - full_noise
    pre = (
        jnp.dot(mixed, w_in, precision=highest, preferred_element_type=jnp.float32)
        + fraction[:, None] * time_gain[None, :]
    )
    sigma = jax.nn.sigmoid(pre)
    hidden = pre * sigma
    part_out = jnp.dot(hidden, w_out, precision=highest, preferred_element_type=jnp.float32)
    out = lax.psum(part_out, "col")
    diff = out - velocity
    squared = jnp.sum(diff * diff)
    slope = diff / jnp.sqrt(jnp.float32(noise_count))
    local_out = lax.dot_general(
        hidden,
        slope,
        (((0,), (0,)), ((), ())),
        precision=highest,
        preferred_element_type=jnp.float32,
    )
    back = lax.dot_general(
        slope,
        w_out,
        (((1,), (1,)), ((), ())),
        precision=highest,
        preferred_element_type=jnp.float32,
    )
    dpre = back * sigma * (1.0 + pre * (1.0 - sigma))
    local_in = lax.dot_general(
        mixed, dpre, (((0,), (0,)), ((), ())), precision=highest, preferred_element_type=jnp.float32
    )
    local_time = jnp.sum(fraction[:, None] * dpre, axis=0)
    grad_in, grad_out = (
        lax.psum_scatter(local_in, "row", scatter_dimension=0, tiled=True),
        lax.psum_scatter(local_out, "row", scatter_dimension=1, tiled=True),
    )
    grad_time, squared_all = lax.psum((local_time, squared), "row")
    mse = squared_all / (noise_count * width)
    return (targets, row_pot, col_pot, grad_in, grad_time, grad_out, mse)


def solution(mesh):
    placed = (P("row", "col"), P("col", "row"), P("row"), P(None, "col"), P("col"), P("col", None))
    return jax.shard_map(
        body,
        mesh=mesh,
        in_specs=placed,
        out_specs=(
            P("row", "col"),
            P("row"),
            P("col"),
            P("row", "col"),
            P("col"),
            P("col", "row"),
            P(),
        ),
        check_vma=False,
    )
```

profile of v0, /device:TPU:0, one launch (start us, length us, event | category | flops | bytes accessed | tf_op | source)
XLA Modules:
  0.0 786.1 jit_solution(18099109052659360453)
XLA Ops:
  8.7 68.3 %all-gather.23.cloned.1.call-done = f32[512,3072]{1,0:T(8,128)} async-done(((f32[512,384]{1,0:T(8,128)}), f32[512,3072]{1,0:T(8,128)}) %all-gather.23.cloned.1.call-update) | async-done | bytes 6291472 | tf_op jit(solution)/shard_map/all_gather | solution.py:47
  77.0 3.3 multiply_reduce_fusion.2
  80.3 93.5 %all-gather.25.cloned.1.call-done = f32[768,3072]{1,0:T(8,128)} async-done(((f32[768,768]{1,0:T(8,128)}), f32[768,3072]{1,0:T(8,128)}) %all-gather.25.cloned.1.call-update) | async-done | bytes 9437200 | tf_op jit(solution)/shard_map/all_gather | solution.py:48
  173.8 4.5 multiply_reduce_fusion
  178.3 1.0 copy-done
  179.2 18.3 %subtract_reduce_fusion.3 = (f32[512]{0:T(512)S(1)}, f32[512,768]{1,0:T(8,128)S(1)}) fusion(f32[512,3072]{1,0:T(8,128)S(1)} %copy-done, f32[768,3072]{1,0:T(8,128)} %all-gather.25.cloned.1.call-done, f32[768]{0:T(1024)S(1)} %multiply_reduce_fusion, f32[512]{0:T(512)S(1)} %multiply_reduce_fusion.2), kind=kOutput, calls=%fused_computation.38 | convolution fusion | flops 14497873920 | bytes 17308672 | tf_op jit(solution)/shard_map/dot_general | solution.py:54
  197.9 12.8 %all-gather.11 = f32[8,1,512]{2,1,0:T(1,128)S(1)} all-gather(f32[1,1,512]{2,1,0:T(1,128)S(1)} %bitcast.95), channel_id=3, replica_groups=mesh['row'=4,'col'=8] {'col'}, dimensions={0}, use_global_device_ids=true | all-gather | bytes 18432 | tf_op jit(solution)/shard_map/all_gather | solution.py:14
  210.8 12.8 %all-gather.10 = f32[8,1,512]{2,1,0:T(1,128)S(1)} all-gather(f32[1,1,512]{2,1,0:T(1,128)S(1)} %bitcast.93), channel_id=2, replica_groups=mesh['row'=4,'col'=8] {'col'}, dimensions={0}, use_global_device_ids=true | all-gather | bytes 18432 | tf_op jit(solution)/shard_map/all_gather | solution.py:14
  224.5 8.1 %all-gather.13 = f32[4,1,768]{2,1,0:T(1,128)S(1)} all-gather(f32[1,1,768]{2,1,0:T(1,128)S(1)} %reshape.65), channel_id=5, replica_groups=mesh['row'=4,'col'=8] {'row'}, dimensions={0}, use_global_device_ids=true | all-gather | bytes 15360 | tf_op jit(solution)/shard_map/all_gather | solution.py:14
  232.6 7.2 all-gather.12
  240.7 12.8 %all-gather.15 = f32[8,1,512]{2,1,0:T(1,128)S(1)} all-gather(f32[1,1,512]{2,1,0:T(1,128)S(1)} %bitcast.94), channel_id=7, replica_groups=mesh['row'=4,'col'=8] {'col'}, dimensions={0}, use_global_device_ids=true | all-gather | bytes 18432 | tf_op jit(solution)/shard_map/all_gather | solution.py:14
  253.5 12.8 %all-gather.14 = f32[8,1,512]{2,1,0:T(1,128)S(1)} all-gather(f32[1,1,512]{2,1,0:T(1,128)S(1)} %bitcast.91), channel_id=6, replica_groups=mesh['row'=4,'col'=8] {'col'}, dimensions={0}, use_global_device_ids=true | all-gather | bytes 18432 | tf_op jit(solution)/shard_map/all_gather | solution.py:14
  267.2 8.1 %all-gather.17 = f32[4,1,768]{2,1,0:T(1,128)S(1)} all-gather(f32[1,1,768]{2,1,0:T(1,128)S(1)} %reshape.73), channel_id=9, replica_groups=mesh['row'=4,'col'=8] {'row'}, dimensions={0}, use_global_device_ids=true | all-gather | bytes 15360 | tf_op jit(solution)/shard_map/all_gather | solution.py:14
  275.4 18.3 %all-gather.16 = f32[4,1,768]{2,1,0:T(1,128)S(1)} all-gather(f32[1,1,768]{2,1,0:T(1,128)S(1)} %reshape.71), channel_id=8, replica_groups=mesh['row'=4,'col'=8] {'row'}, dimensions={0}, use_global_device_ids=true | all-gather | bytes 15360 | tf_op jit(solution)/shard_map/all_gather | solution.py:14
  294.6 12.8 %all-gather.19 = f32[8,1,512]{2,1,0:T(1,128)S(1)} all-gather(f32[1,1,512]{2,1,0:T(1,128)S(1)} %bitcast.96), channel_id=11, replica_groups=mesh['row'=4,'col'=8] {'col'}, dimensions={0}, use_global_device_ids=true | all-gather | bytes 18432 | tf_op jit(solution)/shard_map/all_gather | solution.py:14
  307.3 12.8 %all-gather.18 = f32[8,1,512]{2,1,0:T(1,128)S(1)} all-gather(f32[1,1,512]{2,1,0:T(1,128)S(1)} %bitcast.92), channel_id=10, replica_groups=mesh['row'=4,'col'=8] {'col'}, dimensions={0}, use_global_device_ids=true | all-gather | bytes 18432 | tf_op jit(solution)/shard_map/all_gather | solution.py:14
  320.5 19.3 %fusion.6 = f32[512,3072]{1,0:T(8,128)} fusion(f32[768,3072]{1,0:T(8,128)} %all-gather.25.cloned.1.call-done, f32[512,768]{1,0:T(8,128)S(1)} %get-tuple-element.759, f32[512]{0:T(512)S(1)} %log_add_fusion, f32[768]{0:T(1024)S(1)} %add_subtract_fusion), kind=kOutput, calls=%fused_computation.26 | convolution fusion | flops 14496301056 | bytes 17306624 | tf_op jit(solution)/shard_map/dot_general | solution.py:72
  340.4 133.1 %all-reduce.4.cloned.1.call-done = f32[512,3072]{1,0:T(8,128)} async-done(((f32[512,3072]{1,0:T(8,128)}), f32[512,3072]{1,0:T(8,128)}) %all-reduce.4.cloned.1.call-update) | async-done | bytes 6291472 | tf_op jit(solution)/shard_map/psum | solution.py:77
  473.6 14.6 %convolution_add_fusion = f32[512,384]{1,0:T(8,128)S(1)} fusion(f32[3072,384]{1,0:T(8,128)} %param.19, f32[384]{0:T(512)S(1)} %copy-done.7, f32[512]{0:T(512)S(1)} %get-tuple-element.757, f32[512,3072]{1,0:T(8,128)} %all-reduce.4.cloned.1.call-done, f32[512,3072]{1,0:T(8,128)} %all-gather.23.cloned.1.call-done, f32[512]{0:T(512)S(1)} %get-tuple-element.756), kind=kOutput, calls=%fused_computation.43 | convolution fusion | flops 7252869120 | bytes 18093568 | tf_op jit(solution)/shard_map/dot_general | solution.py:83
  488.2 0.9 copy-done.2
  489.1 12.0 %fusion.20 = f32[512,3072]{1,0:T(8,128)} fusion(f32[384,3072]{1,0:T(8,128)S(1)} %bitcast.68, f32[512,384]{1,0:T(8,128)S(1)} %convolution_add_fusion), kind=kOutput, calls=%fused_computation.49 | convolution fusion | flops 7248543744 | bytes 11796480 | tf_op jit(solution)/shard_map/dot_general | solution.py:88
  501.4 136.0 %all-reduce.6.cloned.1.call-done = f32[512,3072]{1,0:T(8,128)} async-done(((f32[512,3072]{1,0:T(8,128)}), f32[512,3072]{1,0:T(8,128)}) %all-reduce.6.cloned.1.call-update) | async-done | bytes 6291472 | tf_op jit(solution)/shard_map/psum | solution.py:89
  637.3 9.5 %multiply_reduce_fusion.1 = (f32[]{:T(128)}, f32[512,3072]{1,0:T(8,128)S(1)}) fusion(f32[512,3072]{1,0:T(8,128)} %all-reduce.6.cloned.1.call-done, f32[512,3072]{1,0:T(8,128)} %all-reduce.4.cloned.1.call-done, f32[512,3072]{1,0:T(8,128)} %all-gather.23.cloned.1.call-done), kind=kLoop, calls=%fused_computation.16 | loop fusion | flops 6291455 | bytes 25165828 | tf_op jit(solution)/shard_map/reduce_sum | solution.py:91
  646.8 2.6 copy-done.1
  649.4 10.6 %fusion = f32[384,3072]{1,0:T(8,128)} fusion(f32[512,3072]{1,0:T(8,128)S(1)} %get-tuple-element.745, f32[512,384]{1,0:T(8,128)} %copy-done.2), kind=kOutput, calls=%fused_computation.20 | convolution fusion | flops 7250116608 | bytes 11796480 | tf_op jit(solution)/shard_map/dot_general | solution.py:93
  660.4 0.8 copy-done.3
  661.2 14.1 %multiply_reduce_fusion.3 = (f32[384]{0:T(512)S(1)}, f32[512,384]{1,0:T(8,128)S(1)}) fusion(f32[512]{0:T(512)S(1)} %get-tuple-element.757, f32[512,384]{1,0:T(8,128)S(1)} %copy-done.3, f32[384,3072]{1,0:T(8,128)} %param.21, f32[512,3072]{1,0:T(8,128)} %copy-done.1), kind=kOutput, calls=%fused_computation.44 | convolution fusion | flops 7251295744 | bytes 12586496 | tf_op jit(solution)/shard_map/dot_general | solution.py:100
  675.3 15.4 %fusion.26 = f32[3072,384]{1,0:T(8,128)} fusion(f32[512,384]{1,0:T(8,128)S(1)} %get-tuple-element.761, f32[512,3072]{1,0:T(8,128)} %all-reduce.4.cloned.1.call-done, f32[512,3072]{1,0:T(8,128)} %all-gather.23.cloned.1.call-done, f32[512]{0:T(512)S(1)} %get-tuple-element.757, f32[512]{0:T(512)S(1)} %get-tuple-element.756), kind=kOutput, calls=%fused_computation.76 | convolution fusion | flops 7252475904 | bytes 18092032 | tf_op jit(solution)/shard_map/dot_general | solution.py:108
  690.7 2.1 constant_dynamic-slice_fusion.6
  692.8 10.5 %all-reduce = (f32[384]{0:T(512)}, f32[]{:T(128)}) all-reduce(f32[384]{0:T(512)S(1)} %get-tuple-element.760, f32[]{:T(128)} %get-tuple-element.744), channel_id=1, replica_groups=mesh['row'=4,'col'=8] {'row'}, use_global_device_ids=true, to_apply=%region_26.0 | all-reduce | flops 385 | bytes 3080 | tf_op jit(solution)/shard_map/psum | solution.py:116
  703.9 13.4 %reduce-scatter.5.cloned.1.call-done = f32[384,768]{1,0:T(8,128)} async-done(((f32[384,3072]{1,0:T(8,128)}), f32[384,768]{1,0:T(8,128)}) %reduce-scatter.5.cloned.1.call-update) | async-done | bytes 1179664 | tf_op jit(solution)/shard_map/reduce_scatter | solution.py:114
  717.3 60.4 %reduce-scatter.3.cloned.1.call-done = f32[768,384]{1,0:T(8,128)} async-done(((f32[3072,384]{1,0:T(8,128)}), f32[768,384]{1,0:T(8,128)}) %reduce-scatter.3.cloned.1.call-update) | async-done | bytes 1179664 | tf_op jit(solution)/shard_map/reduce_scatter | solution.py:113
  (127 shorter events, 8.0 us)
Async XLA Ops:
  7.2 69.9 %all-gather.23.cloned.1.call-start = ((), (), s32[]{:S(2)}) async-start(), calls=%async_computation.2 | async-start | bytes 7077888 | tf_op jit(solution)/shard_map/all_gather | solution.py:47
  7.9 165.9 %all-gather.25.cloned.1.call-start = ((), (), s32[]{:S(2)}) async-start(), calls=%async_computation.3 | async-start | bytes 11796480 | tf_op jit(solution)/shard_map/all_gather | solution.py:48
  8.6 464.9 %all-reduce.4.cloned.1.call-start = ((), (), s32[]{:S(2)}) async-start(), calls=%async_computation.4 | async-start | bytes 12582912 | tf_op jit(solution)/shard_map/psum | solution.py:77
  173.8 5.5 copy-start
  266.7 73.1 %copy-start.5 = (f32[512]{0:T(512)}, f32[512]{0:T(512)S(1)}, u32[]{:S(2)}) copy-start(f32[512]{0:T(512)S(1)} %add_subtract_fusion.2) | copy-start | bytes 6148
  293.9 45.8 %copy-start.4 = (f32[768]{0:T(1024)}, f32[768]{0:T(1024)S(1)}, u32[]{:S(2)}) copy-start(f32[768]{0:T(1024)S(1)} %add_subtract_fusion) | copy-start | bytes 9220
  339.8 0.7 copy-start.6
  339.8 133.8 %copy-start.7 = (f32[384]{0:T(512)S(1)}, f32[384]{0:T(512)}, u32[]{:S(2)}) copy-start(f32[384]{0:T(512)} %param.20) | copy-start | bytes 4612
  339.8 149.3 %slice-start = ((s8[4718592]{0:T(1024)(128)(4,1)}), s8[524288]{0:T(1024)(128)(4,1)S(1)}, s32[]{:S(2)}) async-start(s8[4718592]{0:T(1024)(128)(4,1)} %bitcast.67), calls=%async_computation.8 | async-start | bytes 1048576
  339.8 297.5 %all-reduce.6.cloned.1.call-start = ((), (), s32[]{:S(2)}) async-start(), calls=%async_computation.5 | async-start | bytes 12582912 | tf_op jit(solution)/shard_map/psum | solution.py:89
  473.6 15.5 %slice-start.1 = ((s8[4718592]{0:T(1024)(128)(4,1)}), s8[4194304]{0:T(1024)(128)(4,1)S(1)}, s32[]{:S(2)}) async-start(s8[4718592]{0:T(1024)(128)(4,1)} %bitcast.67), calls=%async_computation.9 | async-start | bytes 8388608
  488.2 0.9 copy-start.2
  501.1 216.2 %reduce-scatter.5.cloned.1.call-start = ((), (), s32[]{:S(2)}) async-start(), calls=%async_computation.7 | async-start | bytes 5898240 | tf_op jit(solution)/shard_map/reduce_scatter | solution.py:114
  646.8 2.6 copy-start.1
  660.1 1.1 copy-start.3
  660.1 117.6 %reduce-scatter.3.cloned.1.call-start = ((), (), s32[]{:S(2)}) async-start(), calls=%async_computation.6 | async-start | bytes 5898240 | tf_op jit(solution)/shard_map/reduce_scatter | solution.py:113
Sparse Core Ops, SparseCore 0:
  9.6 67.4 all-gather.22
  78.9 94.8 all-gather.24
  339.9 133.6 all-reduce.3
  501.2 136.0 all-reduce.5
  660.2 57.0 reduce-scatter.4
  720.7 56.9 reduce-scatter.2
where the time goes:
time: 794 us; the launch traced here: 786 us
  waiting for transfers between devices  506 us (64%)
  blocking collectives  129 us (16%)
  matrix products  104 us (13%)
  other arithmetic  20.5 us (3%)
  between operations  16.6 us (2%)
  local copies, waits for them, and re-layouts  8.41 us (1%)
    psum x1, waiting for transfers between devices, body(): out = lax.psum(part_out, 'col')  136 us
    psum x1, waiting for transfers between devices, body(): whole_targets = lax.psum(partial_value, 'col')  133 us
    all_gather x10, blocking collectives, merged(): everything = jax.tree.map(lambda part: lax.all_gather(part, axis), array)  118 us
    all_gather x1, waiting for transfers between devices, body(): full_images = lax.all_gather(images, 'row', axis=1, tiled=True)  93.5 us
    all_gather x1, waiting for transfers between devices, body(): full_noise = lax.all_gather(noise, 'col', axis=1, tiled=True)  68.3 us
    reduce_scatter x1, waiting for transfers between devices, body(): lax.psum_scatter(local_in, 'row', scatter_dimension=0, tiled=True)  60.4 us
    dot_general x1, matrix products, body(): jnp.dot(weights, full_images, precision=highest, preferred_element_type=j...  19.3 us
    dot_general x1, matrix products, body(): lax.dot_general(full_noise, full_images, (((1,), (1,)), ((), ())), precis...  18.3 us
  transfers between devices with their start and end apart: 6, of which 6 were waited for; matrix products, arithmetic and copies ran while one was open for 4% of the time, Pallas kernels for 0%

commit v1 on v0

v1 whole, which is shorter than its diff:
```python
import functools

import jax
import jax.numpy as jnp
from jax import lax
from jax.experimental import pallas as pl
from jax.experimental.pallas import tpu as pltpu
from jax.sharding import PartitionSpec as P

ITERS = 2
TIMES = 1000


EPSILON = 0.01
MESH = pl.DeviceIdType.MESH
VMEM_LIMIT = 60 * 1024 * 1024


def params(collective_id):
    return pltpu.CompilerParams(
        collective_id=collective_id, has_side_effects=True, vmem_limit_bytes=VMEM_LIMIT
    )


def remote(src, dst, send_sem, recv_sem, device):
    return pltpu.make_async_remote_copy(
        src_ref=src,
        dst_ref=dst,
        send_sem=send_sem,
        recv_sem=recv_sem,
        device_id=device,
        device_id_type=MESH,
    )


def flip(index):
    return index + 1 - 2 * lax.rem(index, 2)


def greet(devices):
    barrier = pltpu.get_barrier_semaphore()
    for device, condition in devices:
        def signal(device=device):
            pl.semaphore_signal(barrier, inc=1, device_id=device, device_id_type=MESH)
        if condition is None:
            signal()
        else:
            pl.when(condition)(signal)
    count = jnp.int32(0)
    for device, condition in devices:
        count = count + (1 if condition is None else jnp.where(condition, 1, 0))
    pl.semaphore_wait(barrier, count)


def gather_kernel(
    rows, chips, noise, images, all_noise, all_images,
    own_sem, right_send, right_recv, left_send, left_recv, pair_send, pair_recv, row_send, row_recv,
):
    r = lax.axis_index("row")
    c = lax.axis_index("col")
    z = c // 2
    core = lax.rem(c, 2)
    width = noise.shape[1]
    height, depth = images.shape
    half = height // 2

    def at(row, col):
        return {"row": row, "col": col}

    partner = at(r, flip(c))
    up = at(r, lax.rem(c + 2, 2 * chips))
    down = at(r, lax.rem(c + 2 * chips - 2, 2 * chips))
    others = [lax.rem(r + k, rows) for k in range(1, rows)]
    greet(
        [(partner, None), (up, z < chips - 1), (down, z > 0)]
        + [(at(other, c), None) for other in others]
    )

    def noise_slot(chip, parity):
        if len(all_noise.shape) == 3:
            return all_noise.at[chip * 2 + parity]
        start = pl.multiple_of((chip * 2 + parity) * width, width)
        return all_noise.at[:, pl.ds(start, width)]

    def image_slot(owner, first, count):
        start = pl.multiple_of(owner * depth, depth)
        return all_images.at[pl.ds(first, count), pl.ds(start, depth)]

    def go_up(src, s):
        chip = z - s
        return remote(src, noise_slot(chip, core), right_send.at[s], right_recv.at[s], up)

    def go_down(src, s):
        chip = z + s
        return remote(src, noise_slot(chip, core), left_send.at[s], left_recv.at[s], down)

    def go_pair(src, chip):
        return remote(src, noise_slot(chip, core), pair_send.at[chip], pair_recv.at[chip], partner)

    own_noise = pltpu.make_async_copy(noise, noise_slot(z, core), own_sem.at[0])
    own_images = pltpu.make_async_copy(images, image_slot(r, 0, height), own_sem.at[1])

    pl.when(z < chips - 1)(lambda: go_up(noise, 0).start())
    pl.when(z > 0)(lambda: go_down(noise, 0).start())

    if rows == 4:
        xn = flip(r)
        yn = lax.rem(r + 2, 4)
        dg = flip(yn)
        to_x, to_y = at(xn, c), at(yn, c)

        def part(src_ref, owner, second, k, target):
            first = half if second else 0
            src = images.at[pl.ds(first, half), :] if src_ref is None else image_slot(owner, first, half)
            return remote(
                src, image_slot(owner, first, half), row_send.at[k], row_recv.at[k], target
            )

        first_x, first_y = part(None, r, False, 0, to_x), part(None, r, True, 1, to_y)
        second_x, second_y = part(None, r, True, 2, to_x), part(None, r, False, 3, to_y)
        first_x.start()
        first_y.start()
        second_x.start()
        second_y.start()
        pass_y, pass_x = part(0, xn, False, 4, to_y), part(0, yn, True, 5, to_x)
        in_first_x, in_first_y = part(None, xn, False, 0, to_x), part(None, yn, True, 1, to_y)
        in_second_x, in_second_y = part(None, xn, True, 2, to_x), part(None, yn, False, 3, to_y)
        in_pass_y, in_pass_x = part(None, dg, False, 4, to_y), part(None, dg, True, 5, to_x)
    else:
        sends = [
            remote(images, image_slot(r, 0, height), row_send.at[k], row_recv.at[k], at(other, c))
            for k, other in enumerate(others)
        ]
        for copy in sends:
            copy.start()

    own_noise.start()
    own_images.start()
    go_pair(noise, z).start()

    for s in range(chips - 1):
        from_down = z - 1 - s >= 0
        from_up = z + 1 + s < chips

        def arrived_up(s=s):
            chip = z - 1 - s
            remote(noise, noise_slot(chip, core), right_send.at[s], right_recv.at[s], up).wait_recv()
            if s + 1 < chips - 1:
                pl.when(z < chips - 1)(lambda: go_up(noise_slot(chip, core), s + 1).start())
            go_pair(noise_slot(chip, core), chip).start()

        def arrived_down(s=s):
            chip = z + 1 + s
            remote(noise, noise_slot(chip, core), left_send.at[s], left_recv.at[s], down).wait_recv()
            if s + 1 < chips - 1:
                pl.when(z > 0)(lambda: go_down(noise_slot(chip, core), s + 1).start())
            go_pair(noise_slot(chip, core), chip).start()

        pl.when(from_down)(arrived_up)
        pl.when(from_up)(arrived_down)
        if rows == 4 and s == min(1, chips - 2):
            in_first_x.wait_recv()
            pass_y.start()
            in_first_y.wait_recv()
            pass_x.start()

    if rows == 4:
        for copy in (in_second_x, in_second_y, in_pass_y, in_pass_x):
            copy.wait_recv()
        for copy in (first_x, first_y, second_x, second_y, pass_y, pass_x):
            copy.wait_send()
    else:
        for k, other in enumerate(others):
            source = lax.rem(r + rows - 1 - k, rows)
            remote(
                images, image_slot(source, 0, height), row_send.at[k], row_recv.at[k], at(other, c)
            ).wait_recv()
        for copy in sends:
            copy.wait_send()

    own_noise.wait()
    own_images.wait()
    for s in range(chips - 1):
        pl.when(jnp.logical_and(z < chips - 1, z - s >= 0))(lambda s=s: go_up(noise, s).wait_send())
        pl.when(jnp.logical_and(z > 0, z + s < chips))(lambda s=s: go_down(noise, s).wait_send())
    for chip in range(chips):
        copy = remote(
            noise, noise_slot(chip, 1 - core), pair_send.at[chip], pair_recv.at[chip], partner
        )
        copy.wait_send()
        copy.wait_recv()


def gathered(noise, images, rows, cols):
    chips = cols // 2
    dma = pltpu.SemaphoreType.DMA
    anywhere = pl.BlockSpec(memory_space=pl.ANY)
    inside = pl.BlockSpec(memory_space=pltpu.VMEM)
    steps = max(chips - 1, 1)
    points, width = noise.shape
    stacked = width % 128 != 0
    full_noise, full_images = pl.pallas_call(
        functools.partial(gather_kernel, rows, chips),
        out_shape=(
            jax.ShapeDtypeStruct(
                (cols, points, width) if stacked else (points, width * cols), jnp.float32
            ),
            jax.ShapeDtypeStruct((images.shape[0], images.shape[1] * rows), jnp.float32),
        ),
        in_specs=[inside, inside],
        out_specs=(anywhere, anywhere),
        scratch_shapes=[
            dma((2,)), dma((steps,)), dma((steps,)), dma((steps,)), dma((steps,)),
            dma((chips,)), dma((chips,)), dma((max(rows, 6),)), dma((max(rows, 6),)),
        ],
        compiler_params=params(0),
        name="gather",
    )(noise, images)
    if stacked:
        full_noise = jnp.swapaxes(full_noise, 0, 1).reshape(points, width * cols)
    return full_noise, full_images


def sinkhorn_kernel(
    rows, cols, noise_count, image_count, scaled, weights, row_out, col_out,
    row_mine, row_all, col_mine, col_all, stat_peak, stat_total, pots,
    row_send, row_recv, col_send, col_recv,
):
    r = lax.axis_index("row")
    c = lax.axis_index("col")
    points, pictures = scaled.shape
    slab = 64
    slabs = points // slab

    def at(row, col):
        return {"row": row, "col": col}

    row_peers = [at(r, lax.rem(c + k, cols)) for k in range(1, cols)]
    col_peers = [at(lax.rem(r + k, rows), c) for k in range(1, rows)]
    greet([(peer, None) for peer in row_peers + col_peers])

    def exchange(mine, everything, send, recv, peers, position, turn):
        count = len(peers) + 1
        copies = [
            remote(mine.at[turn], everything.at[turn, position], send.at[turn, k], recv.at[turn, k], peer)
            for k, peer in enumerate(peers)
        ]
        for copy in copies:
            copy.start()
        for k, peer in enumerate(peers):
            source = lax.rem(position + count - 1 - k, count)
            remote(
                mine.at[turn], everything.at[turn, source], send.at[turn, k], recv.at[turn, k], peer
            ).wait_recv()
        for copy in copies:
            copy.wait_send()
        peak, total = mine[turn, 0:1, :], mine[turn, 1:2, :]
        sources = [lax.rem(position + k, count) for k in range(1, count)]
        pairs = [everything[turn, source] for source in sources]
        top = peak
        for pair in pairs:
            top = jnp.maximum(top, pair[0:1])
        whole = total * jnp.exp(peak - top)
        for pair in pairs:
            whole = whole + pair[1:2] * jnp.exp(pair[0:1] - top)
        return jnp.log(whole) + top

    def over_images(col_pot, turn):
        def step(i, carry):
            window = pl.ds(pl.multiple_of(i * slab, slab), slab)
            logits = col_pot - scaled[window, :]
            peak = jnp.max(logits, axis=1, keepdims=True)
            total = jnp.sum(jnp.exp(logits - peak), axis=1, keepdims=True)
            stat_peak[window, :] = jnp.broadcast_to(peak, (slab, 128))
            stat_total[window, :] = jnp.broadcast_to(total, (slab, 128))
            return carry

        lax.fori_loop(0, slabs, step, 0)
        row_mine[turn, 0:1, :] = stat_peak[...].T[0:1, :]
        row_mine[turn, 1:2, :] = stat_total[...].T[0:1, :]
        return exchange(row_mine, row_all, row_send, row_recv, row_peers, c, turn)

    def as_column(line):
        pots[...] = jnp.broadcast_to(line, (128, points)).T

    def over_noise(turn):
        def top_of(i, peak):
            window = pl.ds(pl.multiple_of(i * slab, slab), slab)
            logits = pots[window, 0:1] - scaled[window, :]
            return jnp.maximum(peak, jnp.max(logits, axis=0, keepdims=True))

        peak = lax.fori_loop(0, slabs, top_of, jnp.full((1, pictures), -jnp.inf, jnp.float32))

        def sum_of(i, total):
            window = pl.ds(pl.multiple_of(i * slab, slab), slab)
            logits = pots[window, 0:1] - scaled[window, :]
            return total + jnp.sum(jnp.exp(logits - peak), axis=0, keepdims=True)

        total = lax.fori_loop(0, slabs, sum_of, jnp.zeros((1, pictures), jnp.float32))
        col_mine[turn, 0:1, :] = peak
        col_mine[turn, 1:2, :] = total
        return exchange(col_mine, col_all, col_send, col_recv, col_peers, r, turn)

    col_pot = jnp.zeros((1, pictures), jnp.float32)
    for turn in range(ITERS):
        row_pot = jnp.log(jnp.float32(image_count)) - over_images(col_pot, turn)
        as_column(row_pot)
        col_pot = jnp.log(jnp.float32(noise_count)) - over_noise(turn)
    row_out[...] = row_pot
    col_out[...] = col_pot
    as_column(over_images(col_pot, ITERS))

    def weigh(i, carry):
        window = pl.ds(pl.multiple_of(i * slab, slab), slab)
        weights[window, :] = jnp.exp(col_pot - scaled[window, :] - pots[window, 0:1])
        return carry

    lax.fori_loop(0, slabs, weigh, 0)


def coupled(scaled, rows, cols):
    points, pictures = scaled.shape
    dma = pltpu.SemaphoreType.DMA
    inside = pl.BlockSpec(memory_space=pltpu.VMEM)
    turns = ITERS + 1
    weights, row_pot, col_pot = pl.pallas_call(
        functools.partial(sinkhorn_kernel, rows, cols, points * rows, pictures * cols),
        out_shape=(
            jax.ShapeDtypeStruct((points, pictures), jnp.float32),
            jax.ShapeDtypeStruct((1, points), jnp.float32),
            jax.ShapeDtypeStruct((1, pictures), jnp.float32),
        ),
        in_specs=[inside],
        out_specs=(inside, inside, inside),
        scratch_shapes=[
            pltpu.VMEM((turns, 2, points), jnp.float32),
            pltpu.VMEM((turns, cols, 2, points), jnp.float32),
            pltpu.VMEM((ITERS, 2, pictures), jnp.float32),
            pltpu.VMEM((ITERS, rows, 2, pictures), jnp.float32),
            pltpu.VMEM((points, 128), jnp.float32),
            pltpu.VMEM((points, 128), jnp.float32),
            pltpu.VMEM((points, 128), jnp.float32),
            dma((turns, cols)), dma((turns, cols)), dma((ITERS, rows)), dma((ITERS, rows)),
        ],
        compiler_params=params(1),
        name="sinkhorn",
    )(scaled)
    return weights, row_pot[0], col_pot[0]


def total_kernel(
    chips, count, part, whole, own, other, going, coming,
    load_sem, keep_sem, pair_send, pair_recv, sum_send, sum_recv,
    cast_send, cast_recv, share_send, share_recv,
):
    r = lax.axis_index("row")
    c = lax.axis_index("col")
    z = c // 2
    core = lax.rem(c, 2)
    points, features = part.shape
    width = features // 2
    tall = points // count
    per_way = count // 2
    last = chips - 1

    def at(col):
        return {"row": r, "col": col}

    partner = at(flip(c))
    up = at(lax.rem(c + 2, 2 * chips))
    down = at(lax.rem(c + 2 * chips - 2, 2 * chips))
    greet([(partner, None), (up, z < last), (down, z > 0)])

    mine = pl.multiple_of(core * width, width)
    theirs = pl.multiple_of((1 - core) * width, width)

    def rows_of(j):
        return pl.ds(pl.multiple_of(j * tall, tall), tall)

    def load(j):
        return pltpu.make_async_copy(
            part.at[rows_of(j), pl.ds(mine, width)], own.at[rows_of(j), :], load_sem.at[j]
        )

    def pair(j):
        return remote(
            part.at[rows_of(j), pl.ds(theirs, width)], other.at[rows_of(j), :],
            pair_send.at[j], pair_recv.at[j], partner,
        )

    def start(j, carry):
        pair(j).start()
        load(j).start()
        return carry

    lax.fori_loop(0, count, start, 0)

    def reduce_step(j, first, final, onward):
        load(j).wait()
        pair(j).wait_recv()
        window = rows_of(j)

        @pl.when(first)
        def _():
            going[window, :] = own[window, :] + other[window, :]

        @pl.when(jnp.logical_not(first))
        def _():
            hop(j, onward).wait_recv()
            going[window, :] = own[window, :] + other[window, :] + coming[window, :]

        @pl.when(jnp.logical_not(final))
        def _():
            hop(j, onward).start()

    def hop(j, target):
        return remote(
            going.at[rows_of(j), :], coming.at[rows_of(j), :], sum_send.at[j], sum_recv.at[j], target
        )

    def spot(j, start_col):
        return whole.at[rows_of(j), pl.ds(start_col, width)]

    def cast(j, target):
        return remote(spot(j, mine), spot(j, mine), cast_send.at[j], cast_recv.at[j], target)

    def cast_first(j, target):
        return remote(going.at[rows_of(j), :], spot(j, mine), cast_send.at[j], cast_recv.at[j], target)

    def share(j):
        return remote(spot(j, mine), spot(j, mine), share_send.at[j], share_recv.at[j], partner)

    def share_first(j):
        return remote(going.at[rows_of(j), :], spot(j, mine), share_send.at[j], share_recv.at[j], partner)

    def keep(j):
        return pltpu.make_async_copy(going.at[rows_of(j), :], spot(j, mine), keep_sem.at[j])

    def way(step, here, parity, onward, back):
        j = step - here

        @pl.when(jnp.logical_and(j >= 0, j < per_way))
        def _():
            index = 2 * j + parity
            reduce_step(index, here == 0, here == last, onward)

            @pl.when(here == last)
            def _():
                cast_first(index, back).start()
                keep(index).start()
                share_first(index).start()

        k = step - (2 * last - here)

        @pl.when(jnp.logical_and(jnp.logical_and(k >= 0, k < per_way), here < last))
        def _():
            index = 2 * k + parity
            cast(index, back).wait_recv()

            @pl.when(here > 0)
            def _():
                cast(index, back).start()

            share(index).start()

    def step(s, carry):
        way(s, z, 0, up, down)
        way(s, last - z, 1, down, up)
        return carry

    lax.fori_loop(0, per_way + 2 * last, step, 0)

    def finish(j, carry):
        pair(j).wait_send()
        share(j).wait_send()
        remote(
            spot(j, mine), spot(j, theirs), share_send.at[j], share_recv.at[j], partner
        ).wait_recv()
        here = jnp.where(lax.rem(j, 2) == 0, z, last - z)

        @pl.when(here < last)
        def _():
            hop(j, partner).wait_send()

        @pl.when(here == last)
        def _():
            keep(j).wait()

        @pl.when(here > 0)
        def _():
            cast(j, partner).wait_send()

        return carry

    lax.fori_loop(0, count, finish, 0)


def total_over_col(part, cols, collective_id):
    points, features = part.shape
    chips = cols // 2
    count = points // 16
    dma = pltpu.SemaphoreType.DMA
    anywhere = pl.BlockSpec(memory_space=pl.ANY)
    return pl.pallas_call(
        functools.partial(total_kernel, chips, count),
        out_shape=jax.ShapeDtypeStruct((points, features), jnp.float32),
        in_specs=[anywhere],
        out_specs=anywhere,
        scratch_shapes=[pltpu.VMEM((points, features // 2), jnp.float32)] * 4 + [dma((count,))] * 10,
        compiler_params=params(collective_id),
        name=f"total{collective_id}",
    )(part)


def body(rows, cols, noise, images, time_index, w_in, time_gain, w_out):
    high = lax.Precision.HIGH
    full_noise, full_images = gathered(noise, images, rows, cols)
    width = full_noise.shape[1]
    noise_count = full_noise.shape[0] * rows
    noise_norms = jnp.sum(full_noise * full_noise, axis=1)
    image_norms = jnp.sum(full_images * full_images, axis=1)
    cross = lax.dot_general(
        full_noise,
        full_images,
        (((1,), (1,)), ((), ())),
        precision=high,
        preferred_element_type=jnp.float32,
    )
    scaled = (noise_norms[:, None] + image_norms[None, :] - 2.0 * cross) / (width * EPSILON)
    weights, row_pot, col_pot = coupled(scaled, rows, cols)
    partial_value = jnp.dot(
        weights, full_images, precision=high, preferred_element_type=jnp.float32
    )
    slice_width = noise.shape[1]
    slice_start = lax.axis_index("col") * slice_width
    whole_targets = total_over_col(partial_value, cols, 2)
    targets = lax.dynamic_slice_in_dim(whole_targets, slice_start, slice_width, 1)
    fraction = (time_index.astype(jnp.float32) + 0.5) / TIMES
    mixed = (1.0 - fraction)[:, None] * full_noise + fraction[:, None] * whole_targets
    velocity = whole_targets - full_noise
    pre = (
        jnp.dot(mixed, w_in, precision=high, preferred_element_type=jnp.float32)
        + fraction[:, None] * time_gain[None, :]
    )
    sigma = jax.nn.sigmoid(pre)
    hidden = pre * sigma
    part_out = jnp.dot(hidden, w_out, precision=high, preferred_element_type=jnp.float32)
    out = total_over_col(part_out, cols, 3)
    diff = out - velocity
    squared = jnp.sum(diff * diff)
    slope = diff / jnp.sqrt(jnp.float32(noise_count))
    local_out = lax.dot_general(
        hidden,
        slope,
        (((0,), (0,)), ((), ())),
        precision=high,
        preferred_element_type=jnp.float32,
    )
    back = lax.dot_general(
        slope,
        w_out,
        (((1,), (1,)), ((), ())),
        precision=high,
        preferred_element_type=jnp.float32,
    )
    dpre = back * sigma * (1.0 + pre * (1.0 - sigma))
    local_in = lax.dot_general(
        mixed, dpre, (((0,), (0,)), ((), ())), precision=high, preferred_element_type=jnp.float32
    )
    local_time = jnp.sum(fraction[:, None] * dpre, axis=0)
    grad_in, grad_out = (
        lax.psum_scatter(local_in, "row", scatter_dimension=0, tiled=True),
        lax.psum_scatter(local_out, "row", scatter_dimension=1, tiled=True),
    )
    grad_time, squared_all = lax.psum((local_time, squared), "row")
    mse = squared_all / (noise_count * width)
    return (targets, row_pot, col_pot, grad_in, grad_time, grad_out, mse)


def solution(mesh):
    placed = (P("row", "col"), P("col", "row"), P("row"), P(None, "col"), P("col"), P("col", None))
    return jax.shard_map(
        functools.partial(body, mesh.shape["row"], mesh.shape["col"]),
        mesh=mesh,
        in_specs=placed,
        out_specs=(
            P("row", "col"),
            P("row"),
            P("col"),
            P("row", "col"),
            P("col"),
            P("col", "row"),
            P(),
        ),
        check_vma=False,
    )
```

time: 794 us -> 511 us (0.64)
  waiting for transfers between devices: 506 us -> 83.9 us
  Pallas kernels: 0 us -> 308 us
  blocking collectives: 129 us -> 10.2 us
  matrix products: 104 us -> 66.6 us
    pallas_call x0 -> x4, Pallas kernels: none -> 308 us  [the longest x2 192 us: total_over_col(): pl.pallas_call(functools.partial(total_kernel, chips, count), out_shape=j...]
    psum x2 -> x0, waiting for transfers between devices: 269 us -> none  [the longest x1 136 us: body(): out = lax.psum(part_out, 'col')]
    all_gather x2 -> x0, waiting for transfers between devices: 162 us -> none  [the longest x1 93.5 us: body(): full_images = lax.all_gather(images, 'row', axis=1, tiled=True)]
    all_gather x10 -> x0, blocking collectives: 118 us -> none  [merged(): everything = jax.tree.map(lambda part: lax.all_gather(part, axis), array)]
    dot_general x6, matrix products: 85.9 us -> 57.5 us  [the longest x1 12.5 us: body(): jnp.dot(weights, full_images, precision=high, preferred_element_type=jnp....]
    reduce_scatter x1, waiting for transfers between devices: 13.4 us -> 23.3 us  [body(): lax.psum_scatter(local_out, 'row', scatter_dimension=1, tiled=True)]
    dot_general x1, matrix products: 18.3 us -> 9.07 us  [body(): lax.dot_general(full_noise, full_images, (((1,), (1,)), ((), ())), precis...]
  transfers between devices with their start and end apart: 6 -> 2, of which waited for: 6 -> 2; matrix products, arithmetic and copies ran while one was open for 4% -> 5% of each run, Pallas kernels for 0% -> 0%
where the time goes in v1:
time: 511 us
  Pallas kernels  308 us (60%)
  waiting for transfers between devices  83.9 us (16%)
  matrix products  66.6 us (13%)
  other arithmetic  18.7 us (4%)
  between operations  16 us (3%)
  blocking collectives  10.2 us (2%)
  local copies, waits for them, and re-layouts  7.87 us (2%)
    pallas_call x2, Pallas kernels, total_over_col(): pl.pallas_call(functools.partial(total_kernel, chips, count), out_shape=j...  192 us
    pallas_call x1, Pallas kernels, gathered(): pl.pallas_call(functools.partial(gather_kernel, rows, chips), out_shape=(...  83.2 us
    reduce_scatter x1, waiting for transfers between devices, body(): lax.psum_scatter(local_in, 'row', scatter_dimension=0, tiled=True)  60.6 us
    pallas_call x1, Pallas kernels, coupled(): pl.pallas_call(functools.partial(sinkhorn_kernel, rows, cols, points * ro...  32.9 us
    reduce_scatter x1, waiting for transfers between devices, body(): lax.psum_scatter(local_out, 'row', scatter_dimension=1, tiled=True)  23.3 us
    dot_general x1, matrix products, body(): jnp.dot(weights, full_images, precision=high, preferred_element_type=jnp....  12.5 us
    dot_general x1, matrix products, body(): lax.dot_general(mixed, dpre, (((0,), (0,)), ((), ())), precision=high, pr...  10.9 us
  transfers between devices with their start and end apart: 2, of which 2 were waited for; matrix products, arithmetic and copies ran while one was open for 5% of the time, Pallas kernels for 0%

profile of v1, /device:TPU:0, one launch (start us, length us, event | category | flops | bytes accessed | tf_op | source)
XLA Modules:
  0.0 511.0 jit_solution(12576486422098210965)
XLA Ops:
  7.2 0.0 reduce-scatter.5.cloned.1.call-start
  7.2 83.2 %gather.1 = (f32[512,3072]{1,0:T(8,128)}, f32[768,3072]{1,0:T(8,128)}) custom-call(f32[512,384]{1,0:T(8,128)} %noise.1, f32[768,768]{1,0:T(8,128)} %images.1), custom_call_target="tpu_custom_call" | custom-call | tf_op jit(solution)/shard_map/gather/pallas_call | solution.py:202
  90.4 0.0 slice-start
  90.4 3.4 multiply_reduce_fusion.2
  93.9 5.2 %multiply_reduce_fusion = f32[768]{0:T(1024)S(1)} fusion(f32[768,3072]{1,0:T(8,128)} %get-tuple-element.13), kind=kLoop, calls=%fused_computation | loop fusion | flops 4717824 | bytes 9440256 | tf_op jit(solution)/shard_map/reduce_sum | solution.py:521
  99.0 0.8 copy-done.1
  99.9 0.8 slice-done.1
  100.7 9.1 %subtract_multiply_fusion.scaled = f32[512,768]{1,0:T(8,128)} fusion(f32[512,3072]{1,0:T(8,128)S(1)} %bitcast.10, f32[768,3072]{1,0:T(8,128)S(1)} %copy-done.1, f32[768]{0:T(1024)S(1)} %multiply_reduce_fusion, f32[512]{0:T(512)S(1)} %multiply_reduce_fusion.2), kind=kOutput, calls=%fused_computation.11 | convolution fusion | flops 7249330176 | bytes 17306624 | tf_op jit(solution)/shard_map/dot_general | solution.py:522
  109.7 32.9 %sinkhorn.1 = (f32[512,768]{1,0:T(8,128)}, f32[1,512]{1,0:T(1,128)}, f32[1,768]{1,0:T(1,128)}) custom-call(f32[512,768]{1,0:T(8,128)} %subtract_multiply_fusion.scaled), custom_call_target="tpu_custom_call" | custom-call | tf_op jit(solution)/shard_map/sinkhorn/pallas_call | solution.py:326
  142.6 12.5 %fusion.21.part = f32[512,3072]{1,0:T(8,128)} fusion(f32[512,768]{1,0:T(8,128)} %get-tuple-element.14, f32[768,3072]{1,0:T(8,128)} %get-tuple-element.13), kind=kOutput, calls=%fused_computation.27 | convolution fusion | flops 7247757312 | bytes 17301504 | tf_op jit(solution)/shard_map/dot_general | solution.py:531
  155.1 95.4 %total2.1 = f32[512,3072]{1,0:T(8,128)} custom-call(f32[512,3072]{1,0:T(8,128)} %fusion.21.part), custom_call_target="tpu_custom_call" | custom-call | tf_op jit(solution)/shard_map/total2/pallas_call | solution.py:504
  250.6 0.0 slice-start.3
  250.6 10.1 %convolution_add_fusion = f32[512,384]{1,0:T(8,128)S(1)} fusion(f32[3072,384]{1,0:T(8,128)} %param.9, f32[384]{0:T(512)S(1)} %copy-done.6, f32[512]{0:T(512)S(1)} %get-tuple-element.22, f32[512,3072]{1,0:T(8,128)} %total2.1, f32[512,3072]{1,0:T(8,128)} %get-tuple-element.12, f32[512]{0:T(512)S(1)} %get-tuple-element.21), kind=kOutput, calls=%fused_computation.14 | convolution fusion | flops 3628990464 | bytes 18093568 | tf_op jit(solution)/shard_map/dot_general | solution.py:542
  260.7 0.0 copy-start.2
  260.7 0.9 copy-done.2
  261.6 7.1 %fusion.14.part = f32[512,3072]{1,0:T(8,128)} fusion(f32[384,3072]{1,0:T(8,128)S(1)} %bitcast.12, f32[512,384]{1,0:T(8,128)S(1)} %convolution_add_fusion), kind=kOutput, calls=%fused_computation.18 | convolution fusion | flops 3624665088 | bytes 11796480 | tf_op jit(solution)/shard_map/dot_general | solution.py:547
  268.6 96.3 %total3.1 = f32[512,3072]{1,0:T(8,128)} custom-call(f32[512,3072]{1,0:T(8,128)} %fusion.14.part), custom_call_target="tpu_custom_call" | custom-call | tf_op jit(solution)/shard_map/total3/pallas_call | solution.py:504
  364.9 9.5 %multiply_reduce_fusion.1 = (f32[]{:T(128)}, f32[512,3072]{1,0:T(8,128)S(1)}) fusion(f32[512,3072]{1,0:T(8,128)} %total3.1, f32[512,3072]{1,0:T(8,128)} %total2.1, f32[512,3072]{1,0:T(8,128)} %get-tuple-element.12), kind=kLoop, calls=%fused_computation.1 | loop fusion | flops 6291455 | bytes 25165828 | tf_op jit(solution)/shard_map/reduce_sum | solution.py:550
  374.4 2.6 copy-done
  377.0 7.3 %fusion = f32[384,3072]{1,0:T(8,128)} fusion(f32[512,3072]{1,0:T(8,128)S(1)} %get-tuple-element.20, f32[512,384]{1,0:T(8,128)} %copy-done.2), kind=kOutput, calls=%fused_computation.5 | convolution fusion | flops 3626237952 | bytes 11796480 | tf_op jit(solution)/shard_map/dot_general | solution.py:552
  384.4 0.0 reduce-scatter.5.cloned.1.call-update
  384.4 0.0 reduce-scatter.3.cloned.1.call-start
  384.5 9.6 %multiply_reduce_fusion.3 = (f32[384]{0:T(512)S(1)}, f32[512,384]{1,0:T(8,128)S(1)}) fusion(f32[512]{0:T(512)S(1)} %get-tuple-element.22, f32[512,384]{1,0:T(8,128)} %copy-done.2, f32[384,3072]{1,0:T(8,128)} %param.11, f32[512,3072]{1,0:T(8,128)} %copy-done), kind=kOutput, calls=%fused_computation.15 | convolution fusion | flops 3627417088 | bytes 12586496 | tf_op jit(solution)/shard_map/dot_general | solution.py:559
  394.1 10.9 %fusion.20 = f32[3072,384]{1,0:T(8,128)} fusion(f32[512,384]{1,0:T(8,128)S(1)} %get-tuple-element.24, f32[512,3072]{1,0:T(8,128)} %total2.1, f32[512,3072]{1,0:T(8,128)} %get-tuple-element.12, f32[512]{0:T(512)S(1)} %get-tuple-element.22, f32[512]{0:T(512)S(1)} %get-tuple-element.21), kind=kOutput, calls=%fused_computation.26 | convolution fusion | flops 3628597248 | bytes 18092032 | tf_op jit(solution)/shard_map/dot_general | solution.py:567
  405.0 0.0 reduce-scatter.3.cloned.1.call-update
  405.0 10.2 %all-reduce = (f32[384]{0:T(512)}, f32[]{:T(128)}) all-reduce(f32[384]{0:T(512)S(1)} %get-tuple-element.23, f32[]{:T(128)} %get-tuple-element.19), channel_id=1, replica_groups=mesh['row'=4,'col'=8] {'row'}, use_global_device_ids=true, to_apply=%region_4.0 | all-reduce | flops 385 | bytes 3080 | tf_op jit(solution)/shard_map/psum | solution.py:575
  415.9 0.0 copy-done.3
  415.9 0.6 reduce
  416.5 2.1 constant_dynamic-slice_fusion
  418.6 23.3 %reduce-scatter.5.cloned.1.call-done = f32[384,768]{1,0:T(8,128)} async-done(((f32[384,3072]{1,0:T(8,128)}), f32[384,768]{1,0:T(8,128)}) %reduce-scatter.5.cloned.1.call-update) | async-done | bytes 1179664 | tf_op jit(solution)/shard_map/reduce_scatter | solution.py:573
  441.9 60.6 %reduce-scatter.3.cloned.1.call-done = f32[768,384]{1,0:T(8,128)} async-done(((f32[3072,384]{1,0:T(8,128)}), f32[768,384]{1,0:T(8,128)}) %reduce-scatter.3.cloned.1.call-update) | async-done | bytes 1179664 | tf_op jit(solution)/shard_map/reduce_scatter | solution.py:572
  502.4 0.6 copy.14
  (17 shorter events, 0.0 us)
Async XLA Ops:
  7.2 434.7 %reduce-scatter.5.cloned.1.call-start = ((), (), s32[]{:S(2)}) async-start(), calls=%async_computation.3 | async-start | bytes 5898240 | tf_op jit(solution)/shard_map/reduce_scatter | solution.py:573
  90.4 8.6 %slice-start = ((s8[6291456]{0:T(1024)(128)(4,1)}), s8[4194304]{0:T(1024)(128)(4,1)S(1)}, s32[]{:S(2)}) async-start(s8[6291456]{0:T(1024)(128)(4,1)} %bitcast.9), calls=%async_computation.4 | async-start | bytes 8388608
  90.4 9.5 %copy-start.1 = (f32[768,3072]{1,0:T(8,128)S(1)}, f32[768,3072]{1,0:T(8,128)}, u32[]{:S(2)}) copy-start(f32[768,3072]{1,0:T(8,128)} %get-tuple-element.13) | copy-start | bytes 28311556
  93.9 6.8 %slice-start.1 = ((s8[6291456]{0:T(1024)(128)(4,1)}), s8[2097152]{0:T(1024)(128)(4,1)S(1)}, s32[]{:S(2)}) async-start(s8[6291456]{0:T(1024)(128)(4,1)} %bitcast.9), calls=%async_computation.5 | async-start | bytes 4194304
  155.1 95.5 %copy-start.4 = (s32[512]{0:T(512)S(1)}, s32[512]{0:T(512)}, u32[]{:S(2)}) copy-start(s32[512]{0:T(512)} %param.8) | copy-start | bytes 6148
  155.1 95.5 %copy-start.6 = (f32[384]{0:T(512)S(1)}, f32[384]{0:T(512)}, u32[]{:S(2)}) copy-start(f32[384]{0:T(512)} %param.10) | copy-start | bytes 4612
  155.1 106.4 %slice-start.2 = ((s8[4718592]{0:T(1024)(128)(4,1)}), s8[524288]{0:T(1024)(128)(4,1)S(1)}, s32[]{:S(2)}) async-start(s8[4718592]{0:T(1024)(128)(4,1)} %bitcast.11), calls=%async_computation.6 | async-start | bytes 1048576
  250.6 11.0 %slice-start.3 = ((s8[4718592]{0:T(1024)(128)(4,1)}), s8[4194304]{0:T(1024)(128)(4,1)S(1)}, s32[]{:S(2)}) async-start(s8[4718592]{0:T(1024)(128)(4,1)} %bitcast.11), calls=%async_computation.7 | async-start | bytes 8388608
  260.7 0.9 copy-start.2
  374.4 2.6 copy-start
  384.4 118.0 %reduce-scatter.3.cloned.1.call-start = ((), (), s32[]{:S(2)}) async-start(), calls=%async_computation.2 | async-start | bytes 5898240 | tf_op jit(solution)/shard_map/reduce_scatter | solution.py:572
  394.1 21.7 %copy-start.3 = (f32[1,768]{1,0:T(1,128)S(1)}, f32[1,768]{1,0:T(1,128)}, u32[]{:S(2)}) copy-start(f32[1,768]{1,0:T(1,128)} %get-tuple-element.16) | copy-start | bytes 9220
  405.0 97.4 %copy-start.5 = (f32[1,512]{1,0:T(1,128)S(1)}, f32[1,512]{1,0:T(1,128)}, u32[]{:S(2)}) copy-start(f32[1,512]{1,0:T(1,128)} %get-tuple-element.15) | copy-start | bytes 6148
Sparse Core Ops, SparseCore 0:
  384.5 57.3 reduce-scatter.4
  445.4 56.9 reduce-scatter.2

commit v2 on v1

--- a/solution.py
+++ b/solution.py
@@ -12,6 +12,8 @@
 
 
 EPSILON = 0.01
+TALL = 16
+SLACK = 2
 MESH = pl.DeviceIdType.MESH
 VMEM_LIMIT = 60 * 1024 * 1024
 
@@ -349,7 +351,7 @@
 
 
 def total_kernel(
-    chips, count, part, whole, own, other, going, coming,
+    chips, count, slack, part, whole, own, other, going, coming,
     load_sem, keep_sem, pair_send, pair_recv, sum_send, sum_recv,
     cast_send, cast_recv, share_send, share_recv,
 ):
@@ -437,7 +439,7 @@
         return pltpu.make_async_copy(going.at[rows_of(j), :], spot(j, mine), keep_sem.at[j])
 
     def way(step, here, parity, onward, back):
-        j = step - here
+        j = step - slack * here
 
         @pl.when(jnp.logical_and(j >= 0, j < per_way))
         def _():
@@ -450,7 +452,7 @@
                 keep(index).start()
                 share_first(index).start()
 
-        k = step - (2 * last - here)
+        k = step - slack * (2 * last - here)
 
         @pl.when(jnp.logical_and(jnp.logical_and(k >= 0, k < per_way), here < last))
         def _():
@@ -468,7 +470,7 @@
         way(s, last - z, 1, down, up)
         return carry
 
-    lax.fori_loop(0, per_way + 2 * last, step, 0)
+    lax.fori_loop(0, per_way + slack * 2 * last, step, 0)
 
     def finish(j, carry):
         pair(j).wait_send()
@@ -498,11 +500,11 @@
 def total_over_col(part, cols, collective_id):
     points, features = part.shape
     chips = cols // 2
-    count = points // 16
+    count = points // TALL
     dma = pltpu.SemaphoreType.DMA
     anywhere = pl.BlockSpec(memory_space=pl.ANY)
     return pl.pallas_call(
-        functools.partial(total_kernel, chips, count),
+        functools.partial(total_kernel, chips, count, SLACK),
         out_shape=jax.ShapeDtypeStruct((points, features), jnp.float32),
         in_specs=[anywhere],
         out_specs=anywhere,
@@ -510,6 +512,214 @@
         compiler_params=params(collective_id),
         name=f"total{collective_id}",
     )(part)
+
+
+def halves(x):
+    high = x.astype(jnp.bfloat16)
+    return high, (x - high.astype(jnp.float32)).astype(jnp.bfloat16)
+
+
+def three_pass(left, right, dims):
+    left_high, left_low = halves(left)
+    right_high, right_low = halves(right)
+
+    def product(a, b):
+        return lax.dot_general(a, b, (dims, ((), ())), preferred_element_type=jnp.float32)
+
+    return product(left_high, right_high) + (
+        product(left_high, right_low) + product(left_low, right_high)
+    )
+
+
+class Scatter:
+    def __init__(self, rows, r, c, piece, inbox, relay, send, recv):
+        self.rows, self.r, self.c, self.piece = rows, r, c, piece
+        self.inbox, self.relay, self.send, self.recv = inbox, relay, send, recv
+        self.half = inbox.shape[1] // 2
+        self.peers = [{"row": lax.rem(r + k, rows), "col": c} for k in range(1, rows)]
+        if rows == 4:
+            self.xn = flip(r)
+            self.yn = lax.rem(r + 2, 4)
+            self.dg = flip(self.yn)
+            self.to_x = {"row": self.xn, "col": c}
+            self.to_y = {"row": self.yn, "col": c}
+
+    def copy(self, k):
+        first, second = pl.ds(0, self.half), pl.ds(self.half, self.half)
+        src, dst, target = (
+            (lambda: self.piece(self.dg, first), self.relay.at[0], self.to_x),
+            (lambda: self.piece(self.dg, second), self.relay.at[1], self.to_y),
+            (lambda: self.piece(self.xn, first), self.inbox.at[0, first, :], self.to_x),
+            (lambda: self.piece(self.yn, second), self.inbox.at[1, second, :], self.to_y),
+            (lambda: self.relay.at[0], self.inbox.at[1, first, :], self.to_y),
+            (lambda: self.relay.at[1], self.inbox.at[0, second, :], self.to_x),
+        )[k]
+        return remote(src(), dst, self.send.at[k], self.recv.at[k], target)
+
+    def direct(self, k):
+        owner = lax.rem(self.r + 1 + k, self.rows)
+        return remote(
+            self.piece(owner, pl.ds(0, 2 * self.half)), self.inbox.at[k],
+            self.send.at[k], self.recv.at[k], self.peers[k],
+        )
+
+    def order(self):
+        if self.rows == 4:
+            return [self.dg, self.xn, self.yn, self.r]
+        return [lax.rem(self.r + 1 + k, self.rows) for k in range(self.rows)]
+
+    def ready(self, place):
+        if self.rows == 4:
+            for k in ((0, 1), (2,), (3,), ())[place]:
+                self.copy(k).start()
+        elif place < self.rows - 1:
+            self.direct(place).start()
+
+    def forward(self):
+        if self.rows == 4:
+            first, second = pl.ds(0, self.half), pl.ds(self.half, self.half)
+            self.copy(0).wait_recv()
+            self.relay[0] = self.relay[0] + self.piece(self.yn, first)[...]
+            self.copy(4).start()
+            self.copy(1).wait_recv()
+            self.relay[1] = self.relay[1] + self.piece(self.xn, second)[...]
+            self.copy(5).start()
+
+    def finish(self, out):
+        own = self.piece(self.r, pl.ds(0, 2 * self.half))
+        if self.rows == 4:
+            for k in (2, 3, 4, 5):
+                self.copy(k).wait_recv()
+            out[...] = own[...] + self.inbox[0] + self.inbox[1]
+            for k in range(6):
+                self.copy(k).wait_send()
+        else:
+            for k in range(self.rows - 1):
+                self.direct(k).wait_recv()
+            out[...] = own[...]
+            for k in range(self.rows - 1):
+                out[...] = out[...] + self.inbox[k]
+            for k in range(self.rows - 1):
+                self.direct(k).wait_send()
+
+
+def backward_kernel(
+    rows, fraction, pre, squared, local_out, slope, w_out, mixed, grad_in, grad_out, grad_time, error,
+    local_out_in, slope_in, w_out_in, mixed_in, local_in, back,
+    out_inbox, out_relay, in_inbox, in_relay, sums,
+    load_sem, out_send, out_recv, in_send, in_recv, sum_send, sum_recv,
+):
+    r = lax.axis_index("row")
+    c = lax.axis_index("col")
+    hidden, features = local_out.shape
+    block = features // rows
+    peers = [{"row": lax.rem(r + k, rows), "col": c} for k in range(1, rows)]
+    greet([(peer, None) for peer in peers])
+
+    loads = [
+        pltpu.make_async_copy(src, dst, load_sem.at[k])
+        for k, (src, dst) in enumerate(
+            ((local_out, local_out_in), (slope, slope_in), (w_out, w_out_in), (mixed, mixed_in))
+        )
+    ]
+    for load in loads:
+        load.start()
+
+    def columns(owner):
+        return pl.ds(pl.multiple_of(owner * block, block), block)
+
+    def out_piece(owner, window):
+        return local_out_in.at[window, columns(owner)]
+
+    def in_piece(owner, window):
+        start = pl.multiple_of(owner * block, block) + window.start
+        return local_in.at[pl.ds(pl.multiple_of(start, 8), window.size), :]
+
+    over_out = Scatter(rows, r, c, out_piece, out_inbox, out_relay, out_send, out_recv)
+    over_in = Scatter(rows, r, c, in_piece, in_inbox, in_relay, in_send, in_recv)
+
+    loads[0].wait()
+    for place in range(rows):
+        over_out.ready(place)
+
+    loads[1].wait()
+    loads[2].wait()
+    back[...] = jnp.zeros_like(back)
+
+    def back_step(k, carry):
+        window = columns(k)
+        back[...] += three_pass(slope_in[:, window], w_out_in[:, window], ((1,), (1,)))
+        return carry
+
+    lax.fori_loop(0, rows, back_step, 0)
+    sigma = 1.0 / (1.0 + jnp.exp(-pre[...]))
+    back[...] = back[...] * sigma * (1.0 + pre[...] * (1.0 - sigma))
+    sums[r, 0:1, :] = jnp.sum(fraction[...] * back[...], axis=0, keepdims=True)
+    sums[r, 1:2, :] = squared[...]
+
+    def share(k, slot):
+        return remote(sums.at[slot], sums.at[slot], sum_send.at[k], sum_recv.at[k], peers[k])
+
+    for k in range(rows - 1):
+        share(k, r).start()
+
+    loads[3].wait()
+    over_out.forward()
+    order = over_in.order()
+    for place in range(rows):
+        owner = order[place]
+        local_in[columns(owner), :] = three_pass(mixed_in[:, columns(owner)], back[...], ((0,), (0,)))
+        over_in.ready(place)
+        if place == rows - 2:
+            over_in.forward()
+    for k in range(rows - 1):
+        share(k, lax.rem(r + rows - 1 - k, rows)).wait_recv()
+    for k in range(rows - 1):
+        share(k, r).wait_send()
+    both = sums[0]
+    for k in range(1, rows):
+        both = both + sums[k]
+    grad_time[...] = both[0:1]
+    error[...] = both[1:2]
+    over_out.finish(grad_out)
+    over_in.finish(grad_in)
+
+
+def gradients(fraction, pre, squared, local_out, slope, w_out, mixed, rows):
+    points, hidden = pre.shape
+    features = mixed.shape[1]
+    block = features // rows
+    dma = pltpu.SemaphoreType.DMA
+    vmem = functools.partial(pltpu.VMEM, dtype=jnp.float32)
+    anywhere = pl.BlockSpec(memory_space=pl.ANY)
+    inside = pl.BlockSpec(memory_space=pltpu.VMEM)
+    boxes = 2 if rows == 4 else rows - 1
+    copies = max(rows, 6)
+
+    def result(*shape):
+        return jax.ShapeDtypeStruct(shape, jnp.float32)
+
+    return pl.pallas_call(
+        functools.partial(backward_kernel, rows),
+        out_shape=(
+            result(block, hidden), result(hidden, block), result(1, hidden), result(1, hidden),
+        ),
+        in_specs=[inside] * 3 + [anywhere] * 4,
+        out_specs=(inside,) * 4,
+        scratch_shapes=[
+            vmem((hidden, features)), vmem((points, features)), vmem((hidden, features)),
+            vmem((points, features)), vmem((features, hidden)), vmem((points, hidden)),
+            vmem((boxes, hidden, block)), vmem((2, hidden // 2, block)),
+            vmem((boxes, block, hidden)), vmem((2, block // 2, hidden)),
+            vmem((rows, 2, hidden)),
+            dma((4,)), dma((copies,)), dma((copies,)), dma((copies,)), dma((copies,)),
+            dma((rows,)), dma((rows,)),
+        ],
+        compiler_params=params(4),
+        name="backward",
+    )(
+        fraction[:, None], pre, jnp.broadcast_to(squared, (1, hidden)), local_out, slope, w_out, mixed
+    )
 
 
 def body(rows, cols, noise, images, time_index, w_in, time_gain, w_out):
@@ -556,25 +766,11 @@
         precision=high,
         preferred_element_type=jnp.float32,
     )
-    back = lax.dot_general(
-        slope,
-        w_out,
-        (((1,), (1,)), ((), ())),
-        precision=high,
-        preferred_element_type=jnp.float32,
-    )
-    dpre = back * sigma * (1.0 + pre * (1.0 - sigma))
-    local_in = lax.dot_general(
-        mixed, dpre, (((0,), (0,)), ((), ())), precision=high, preferred_element_type=jnp.float32
-    )
-    local_time = jnp.sum(fraction[:, None] * dpre, axis=0)
-    grad_in, grad_out = (
-        lax.psum_scatter(local_in, "row", scatter_dimension=0, tiled=True),
-        lax.psum_scatter(local_out, "row", scatter_dimension=1, tiled=True),
-    )
-    grad_time, squared_all = lax.psum((local_time, squared), "row")
-    mse = squared_all / (noise_count * width)
-    return (targets, row_pot, col_pot, grad_in, grad_time, grad_out, mse)
+    grad_in, grad_out, grad_time, squared_all = gradients(
+        fraction, pre, squared, local_out, slope, w_out, mixed, rows
+    )
+    mse = squared_all[0, 0] / (noise_count * width)
+    return (targets, row_pot, col_pot, grad_in, grad_time[0], grad_out, mse)
 
 
 def solution(mesh):

time: 511 us -> 483 us (0.945); the launches traced: 511 us -> 475 us
  waiting for transfers between devices: 83.9 us -> 0 us
  Pallas kernels: 308 us -> 378 us
  matrix products: 66.6 us -> 45.9 us
  other arithmetic: 18.7 us -> 33.4 us
  between operations: 16 us -> 3.03 us
  blocking collectives: 10.2 us -> 0 us
  local copies, waits for them, and re-layouts: 7.87 us -> 14.9 us
    reduce_scatter x2 -> x0, waiting for transfers between devices: 83.9 us -> none  [the longest x1 60.6 us: body(): lax.psum_scatter(local_in, 'row', scatter_dimension=0, tiled=True)]
    pallas_call x2 -> x3, Pallas kernels: 192 us -> 262 us  [the longest x2 177 us: total_over_col(): pl.pallas_call(functools.partial(total_kernel, chips, count, SLACK), out_...]
    dot_general x2 -> x0, matrix products: 20.5 us -> none  [the longest x1 10.9 us: body(): lax.dot_general(mixed, dpre, (((0,), (0,)), ((), ())), precision=high, pr...]
    div x0 -> x1, other arithmetic: none -> 14.3 us  [body(): slope = diff / jnp.sqrt(jnp.float32(noise_count))]
    psum x1 -> x0, blocking collectives: 10.2 us -> none  [body(): grad_time, squared_all = lax.psum((local_time, squared), 'row')]
    reduce_sum x1, other arithmetic: 9.49 us -> 2.21 us  [body(): squared = jnp.sum(diff * diff)]
    add x0 -> x1, other arithmetic: none -> 6.38 us  [body(): (1.0 - fraction)[:, None] * full_noise + fraction[:, None] * whole_targets]
  transfers between devices with their start and end apart: 2 -> 0, of which waited for: 2 -> 0; matrix products, arithmetic and copies ran while one was open for 5% -> 0% of each run, Pallas kernels for 0% -> 0%
where the time goes in v2:
time: 483 us; the launch traced here: 475 us
  Pallas kernels  378 us (78%)
  matrix products  45.9 us (10%)
  other arithmetic  33.4 us (7%)
  local copies, waits for them, and re-layouts  14.9 us (3%)
    pallas_call x2, Pallas kernels, total_over_col(): pl.pallas_call(functools.partial(total_kernel, chips, count, SLACK), out_...  177 us
    pallas_call x1, Pallas kernels, gradients(): pl.pallas_call(functools.partial(backward_kernel, rows), out_shape=(resul...  85.3 us
    pallas_call x1, Pallas kernels, gathered(): pl.pallas_call(functools.partial(gather_kernel, rows, chips), out_shape=(...  83.2 us
    pallas_call x1, Pallas kernels, coupled(): pl.pallas_call(functools.partial(sinkhorn_kernel, rows, cols, points * ro...  33.1 us
    div x1, other arithmetic, body(): slope = diff / jnp.sqrt(jnp.float32(noise_count))  14.3 us
    dot_general x1, matrix products, body(): jnp.dot(weights, full_images, precision=high, preferred_element_type=jnp....  12.5 us
    dot_general x1, matrix products, body(): lax.dot_general(hidden, slope, (((0,), (0,)), ((), ())), precision=high,...  9.83 us

profile of v2, /device:TPU:0, one launch (start us, length us, event | category | flops | bytes accessed | tf_op | source)
XLA Modules:
  0.0 475.5 jit_solution(2442399170631689982)
XLA Ops:
  0.6 83.2 %gather.1 = (f32[512,3072]{1,0:T(8,128)}, f32[768,3072]{1,0:T(8,128)}) custom-call(f32[512,384]{1,0:T(8,128)} %noise.1, f32[768,768]{1,0:T(8,128)} %images.1), custom_call_target="tpu_custom_call" | custom-call | tf_op jit(solution)/shard_map/gather/pallas_call | solution.py:204
  83.8 0.0 slice-start
  83.8 3.4 multiply_reduce_fusion.2
  87.3 5.2 %multiply_reduce_fusion = f32[768]{0:T(1024)S(1)} fusion(f32[768,3072]{1,0:T(8,128)} %get-tuple-element.17), kind=kLoop, calls=%fused_computation | loop fusion | flops 4717824 | bytes 9440256 | tf_op jit(solution)/shard_map/reduce_sum | solution.py:731
  92.4 0.8 copy-done.2
  93.3 0.8 slice-done.1
  94.1 9.0 %subtract_multiply_fusion.scaled = f32[512,768]{1,0:T(8,128)} fusion(f32[512,3072]{1,0:T(8,128)S(1)} %bitcast.11, f32[768,3072]{1,0:T(8,128)S(1)} %copy-done.2, f32[768]{0:T(1024)S(1)} %multiply_reduce_fusion, f32[512]{0:T(512)S(1)} %multiply_reduce_fusion.2), kind=kOutput, calls=%fused_computation.6 | convolution fusion | flops 7249330176 | bytes 17306624 | tf_op jit(solution)/shard_map/dot_general | solution.py:732
  103.1 33.1 %sinkhorn.1 = (f32[512,768]{1,0:T(8,128)}, f32[1,512]{1,0:T(1,128)}, f32[1,768]{1,0:T(1,128)}) custom-call(f32[512,768]{1,0:T(8,128)} %subtract_multiply_fusion.scaled), custom_call_target="tpu_custom_call" | custom-call | tf_op jit(solution)/shard_map/sinkhorn/pallas_call | solution.py:328
  136.2 12.5 %fusion.4.part = f32[512,3072]{1,0:T(8,128)} fusion(f32[512,768]{1,0:T(8,128)} %get-tuple-element.18, f32[768,3072]{1,0:T(8,128)} %get-tuple-element.17), kind=kOutput, calls=%fused_computation.16 | convolution fusion | flops 7247757312 | bytes 17301504 | tf_op jit(solution)/shard_map/dot_general | solution.py:741
  148.7 88.5 %total2.1 = f32[512,3072]{1,0:T(8,128)} custom-call(f32[512,3072]{1,0:T(8,128)} %fusion.4.part), custom_call_target="tpu_custom_call" | custom-call | tf_op jit(solution)/shard_map/total2/pallas_call | solution.py:506
  237.2 0.0 copy-done.5
  237.2 0.0 copy-start.7
  237.2 0.0 slice-start.3
  237.3 6.4 %multiply_add_fusion.mixed = f32[512,3072]{1,0:T(8,128)S(1)} fusion(f32[512,3072]{1,0:T(8,128)} %total2.1, f32[512,3072]{1,0:T(8,128)} %get-tuple-element.16, f32[512]{0:T(512)S(1)} %get-tuple-element.28, f32[512]{0:T(512)S(1)} %get-tuple-element.27), kind=kLoop, calls=%fused_computation.3 | loop fusion | flops 4718592 | bytes 18878464 | tf_op jit(solution)/shard_map/add | solution.py:749
  243.7 2.6 copy-done
  246.3 7.4 %convolution_add_fusion.pre = f32[512,384]{1,0:T(8,128)S(1)} fusion(f32[512,3072]{1,0:T(8,128)S(1)} %multiply_add_fusion.mixed, f32[3072,384]{1,0:T(8,128)} %param.9, f32[384]{0:T(512)S(1)} %copy-done.7, f32[512]{0:T(512)S(1)} %get-tuple-element.28), kind=kOutput, calls=%fused_computation.7 | convolution fusion | flops 3624271872 | bytes 11800064 | tf_op jit(solution)/shard_map/dot_general | solution.py:752
  253.8 0.0 copy-start.3
  253.8 7.2 %fusion.1.part = f32[512,3072]{1,0:T(8,128)} fusion(f32[384,3072]{1,0:T(8,128)S(1)} %bitcast.13, f32[512,384]{1,0:T(8,128)S(1)} %convolution_add_fusion.pre), kind=kOutput, calls=%fused_computation.10 | convolution fusion | flops 3624665088 | bytes 11796480 | tf_op jit(solution)/shard_map/dot_general | solution.py:757
  260.9 88.2 %total3.1 = f32[512,3072]{1,0:T(8,128)} custom-call(f32[512,3072]{1,0:T(8,128)} %fusion.1.part), custom_call_target="tpu_custom_call" | custom-call | tf_op jit(solution)/shard_map/total3/pallas_call | solution.py:506
  349.1 14.3 %broadcast_multiply_fusion = (f32[512,3072]{1,0:T(8,128)}, f32[512,3072]{1,0:T(8,128)}) fusion(f32[512,3072]{1,0:T(8,128)} %total3.1, f32[512,3072]{1,0:T(8,128)} %total2.1, f32[512,3072]{1,0:T(8,128)} %get-tuple-element.16), kind=kLoop, calls=%fused_computation.5 | loop fusion | flops 4718592 | bytes 31457280 | tf_op jit(solution)/shard_map/div | solution.py:761
  363.5 9.8 %fusion.local_out = f32[384,3072]{1,0:T(8,128)} fusion(f32[512,384]{1,0:T(8,128)S(1)} %convolution_add_fusion.pre, f32[512,3072]{1,0:T(8,128)} %get-tuple-element.26), kind=kOutput, calls=%fused_computation.9 | convolution fusion | flops 3626237952 | bytes 11796480 | tf_op jit(solution)/shard_map/dot_general | solution.py:762
  373.3 2.2 multiply_reduce_fusion.1
  375.5 1.2 broadcast_in_dim.5.squared
  376.7 0.9 copy.13.fraction
  377.6 85.3 %backward.1 = (f32[768,384]{1,0:T(8,128)}, f32[384,768]{1,0:T(8,128)}, f32[1,384]{1,0:T(1,128)}, f32[1,384]{1,0:T(1,128)}) custom-call(f32[512,1]{1,0:T(8,128)} %copy.13.fraction, f32[512,384]{1,0:T(8,128)} %copy-done.3, f32[1,384]{1,0:T(1,128)} %broadcast_in_dim.5.squared, f32[384,3072]{1,0:T(8,128)} %fusion.local_out, ...), custom_call_target="tpu_custom_call" | custom-call | tf_op jit(solution)/shard_map/backward/pallas_call | solution.py:702
  462.9 1.2 reduce.1
  464.1 1.2 slice.3
  465.9 2.1 constant_dynamic-slice_fusion
  468.0 0.6 reduce
  468.6 0.6 copy.17
  469.2 2.4 copy.18
  471.5 2.4 copy.19
  (19 shorter events, 0.0 us)
Async XLA Ops:
  83.8 8.6 %slice-start = ((s8[6291456]{0:T(1024)(128)(4,1)}), s8[4194304]{0:T(1024)(128)(4,1)S(1)}, s32[]{:S(2)}) async-start(s8[6291456]{0:T(1024)(128)(4,1)} %bitcast.10), calls=%async_computation | async-start | bytes 8388608
  83.8 9.5 %copy-start.2 = (f32[768,3072]{1,0:T(8,128)S(1)}, f32[768,3072]{1,0:T(8,128)}, u32[]{:S(2)}) copy-start(f32[768,3072]{1,0:T(8,128)} %get-tuple-element.17) | copy-start | bytes 28311556
  87.3 6.8 %slice-start.1 = ((s8[6291456]{0:T(1024)(128)(4,1)}), s8[2097152]{0:T(1024)(128)(4,1)S(1)}, s32[]{:S(2)}) async-start(s8[6291456]{0:T(1024)(128)(4,1)} %bitcast.10), calls=%async_computation.1 | async-start | bytes 4194304
  148.7 88.5 %copy-start.5 = (s32[512]{0:T(512)S(1)}, s32[512]{0:T(512)}, u32[]{:S(2)}) copy-start(s32[512]{0:T(512)} %param.8) | copy-start | bytes 6148
  148.7 105.1 %slice-start.2 = ((s8[4718592]{0:T(1024)(128)(4,1)}), s8[524288]{0:T(1024)(128)(4,1)S(1)}, s32[]{:S(2)}) async-start(s8[4718592]{0:T(1024)(128)(4,1)} %bitcast.12), calls=%async_computation.2 | async-start | bytes 1048576
  237.2 9.0 %copy-start.7 = (f32[384]{0:T(512)S(1)}, f32[384]{0:T(512)}, u32[]{:S(2)}) copy-start(f32[384]{0:T(512)} %param.10) | copy-start | bytes 4612
  237.2 16.5 %slice-start.3 = ((s8[4718592]{0:T(1024)(128)(4,1)}), s8[4194304]{0:T(1024)(128)(4,1)S(1)}, s32[]{:S(2)}) async-start(s8[4718592]{0:T(1024)(128)(4,1)} %bitcast.12), calls=%async_computation.3 | async-start | bytes 8388608
  243.6 2.6 copy-start
  253.8 109.7 %copy-start.3 = (f32[512,384]{1,0:T(8,128)}, f32[512,384]{1,0:T(8,128)S(1)}, u32[]{:S(2)}) copy-start(f32[512,384]{1,0:T(8,128)S(1)} %convolution_add_fusion.pre) | copy-start | bytes 2359300
  363.5 9.8 %copy-start.1 = (f32[512,3072]{1,0:T(8,128)S(1)}, f32[512,3072]{1,0:T(8,128)}, u32[]{:S(2)}) copy-start(f32[512,3072]{1,0:T(8,128)} %get-tuple-element.26) | copy-start | bytes 18874372
  377.6 90.4 %copy-start.4 = (f32[1,768]{1,0:T(1,128)S(1)}, f32[1,768]{1,0:T(1,128)}, u32[]{:S(2)}) copy-start(f32[1,768]{1,0:T(1,128)} %get-tuple-element.20) | copy-start | bytes 9220
  377.6 91.0 %copy-start.6 = (f32[1,512]{1,0:T(1,128)S(1)}, f32[1,512]{1,0:T(1,128)}, u32[]{:S(2)}) copy-start(f32[1,512]{1,0:T(1,128)} %get-tuple-element.19) | copy-start | bytes 6148

commit v3 on v2

--- a/solution.py
+++ b/solution.py
@@ -585,6 +585,35 @@
             self.relay[1] = self.relay[1] + self.piece(self.xn, second)[...]
             self.copy(5).start()
 
+    def ready_for(self, owner):
+        if self.rows == 4:
+            @pl.when(self.dg == owner)
+            def _():
+                self.copy(0).start()
+                self.copy(1).start()
+
+            pl.when(self.xn == owner)(lambda: self.copy(2).start())
+            pl.when(self.yn == owner)(lambda: self.copy(3).start())
+        else:
+            for k in range(self.rows - 1):
+                pl.when(lax.rem(self.r + 1 + k, self.rows) == owner)(lambda k=k: self.direct(k).start())
+
+    def forward_for(self, owner):
+        if self.rows == 4:
+            first, second = pl.ds(0, self.half), pl.ds(self.half, self.half)
+
+            @pl.when(self.yn == owner)
+            def _():
+                self.copy(0).wait_recv()
+                self.relay[0] = self.relay[0] + self.piece(self.yn, first)[...]
+                self.copy(4).start()
+
+            @pl.when(self.xn == owner)
+            def _():
+                self.copy(1).wait_recv()
+                self.relay[1] = self.relay[1] + self.piece(self.xn, second)[...]
+                self.copy(5).start()
+
     def finish(self, out):
         own = self.piece(self.r, pl.ds(0, 2 * self.half))
         if self.rows == 4:
@@ -604,32 +633,133 @@
 
 
 def backward_kernel(
-    rows, fraction, pre, squared, local_out, slope, w_out, mixed, grad_in, grad_out, grad_time, error,
-    local_out_in, slope_in, w_out_in, mixed_in, local_in, back,
+    rows, chips, count, slack, scale, fraction, pre, part, velocity, w_out, mixed,
+    grad_in, grad_out, grad_time, error,
+    own, other, coming, whole, local_out, held, w_out_in, local_in, back, squares,
     out_inbox, out_relay, in_inbox, in_relay, sums,
-    load_sem, out_send, out_recv, in_send, in_recv, sum_send, sum_recv,
+    load_sem, pair_send, pair_recv, sum_send, sum_recv, cast_send, cast_recv, share_send, share_recv,
+    held_sem, w_sem, out_send, out_recv, in_send, in_recv, small_send, small_recv,
 ):
     r = lax.axis_index("row")
     c = lax.axis_index("col")
-    hidden, features = local_out.shape
+    z = c // 2
+    core = lax.rem(c, 2)
+    points, features = part.shape
     block = features // rows
+    per_block = count // rows
+    per_way = count // 2
+    half = points // 2
+    tall = half // per_block
+    last = chips - 1
+
+    def at(col):
+        return {"row": r, "col": col}
+
+    partner = at(flip(c))
+    up = at(lax.rem(c + 2, 2 * chips))
+    down = at(lax.rem(c + 2 * chips - 2, 2 * chips))
     peers = [{"row": lax.rem(r + k, rows), "col": c} for k in range(1, rows)]
-    greet([(peer, None) for peer in peers])
-
-    loads = [
-        pltpu.make_async_copy(src, dst, load_sem.at[k])
-        for k, (src, dst) in enumerate(
-            ((local_out, local_out_in), (slope, slope_in), (w_out, w_out_in), (mixed, mixed_in))
-        )
-    ]
-    for load in loads:
-        load.start()
+    greet([(partner, None), (up, z < last), (down, z > 0)] + [(peer, None) for peer in peers])
 
     def columns(owner):
         return pl.ds(pl.multiple_of(owner * block, block), block)
 
+    def fixed(owner):
+        return pl.ds(owner * block, block)
+
+    def local(ref, j):
+        start = pl.multiple_of(lax.rem(j, per_block) * tall, tall)
+        return ref.at[pl.ds(start, tall), columns(j // per_block)]
+
+    def spot(ref, j, which):
+        start = pl.multiple_of(which * half + lax.rem(j, per_block) * tall, tall)
+        return ref.at[pl.ds(start, tall), columns(j // per_block)]
+
+    def load(j):
+        return pltpu.make_async_copy(spot(part, j, core), local(own, j), load_sem.at[j])
+
+    def pair(j):
+        return remote(
+            spot(part, j, 1 - core), local(other, j), pair_send.at[j], pair_recv.at[j], partner
+        )
+
+    def hop(j, target):
+        return remote(local(own, j), local(coming, j), sum_send.at[j], sum_recv.at[j], target)
+
+    def cast(j, target, src=None):
+        src = spot(whole, j, core) if src is None else src
+        return remote(src, spot(whole, j, core), cast_send.at[j], cast_recv.at[j], target)
+
+    def share(j, src=None):
+        src = spot(whole, j, core) if src is None else src
+        return remote(src, spot(whole, j, core), share_send.at[j], share_recv.at[j], partner)
+
+    def begin(j, carry):
+        pair(j).start()
+        load(j).start()
+        return carry
+
+    lax.fori_loop(0, count, begin, 0)
+
+    def hold(source, owner):
+        return pltpu.make_async_copy(
+            source.at[:, fixed(owner)], held.at[:, fixed(owner)], held_sem.at[owner]
+        )
+
+    for owner in range(rows):
+        hold(velocity, owner).start()
+    w_load = pltpu.make_async_copy(w_out, w_out_in, w_sem.at[0])
+    w_load.start()
+
+    def way(step, here, parity, onward, behind):
+        j = step - slack * here
+
+        @pl.when(jnp.logical_and(j >= 0, j < per_way))
+        def _():
+            index = 2 * j + parity
+            load(index).wait()
+            pair(index).wait_recv()
+            mine = local(own, index)
+
+            @pl.when(here == 0)
+            def _():
+                mine[...] = mine[...] + local(other, index)[...]
+
+            @pl.when(here > 0)
+            def _():
+                hop(index, onward).wait_recv()
+                mine[...] = mine[...] + local(other, index)[...] + local(coming, index)[...]
+
+            @pl.when(here < last)
+            def _():
+                hop(index, onward).start()
+
+            @pl.when(here == last)
+            def _():
+                cast(index, behind, mine).start()
+                share(index, mine).start()
+                spot(whole, index, core)[...] = mine[...]
+
+        k = step - slack * (2 * last - here)
+
+        @pl.when(jnp.logical_and(jnp.logical_and(k >= 0, k < per_way), here < last))
+        def _():
+            index = 2 * k + parity
+            cast(index, behind).wait_recv()
+
+            @pl.when(here > 0)
+            def _():
+                cast(index, behind).start()
+
+            share(index).start()
+
+    def step(s, carry):
+        way(s, z, 0, up, down)
+        way(s, last - z, 1, down, up)
+        return carry
+
     def out_piece(owner, window):
-        return local_out_in.at[window, columns(owner)]
+        return local_out.at[window, columns(owner)]
 
     def in_piece(owner, window):
         start = pl.multiple_of(owner * block, block) + window.start
@@ -638,88 +768,125 @@
     over_out = Scatter(rows, r, c, out_piece, out_inbox, out_relay, out_send, out_recv)
     over_in = Scatter(rows, r, c, in_piece, in_inbox, in_relay, in_send, in_recv)
 
-    loads[0].wait()
-    for place in range(rows):
-        over_out.ready(place)
-
-    loads[1].wait()
-    loads[2].wait()
+    sigma = 1.0 / (1.0 + jnp.exp(-pre[...]))
     back[...] = jnp.zeros_like(back)
-
-    def back_step(k, carry):
-        window = columns(k)
-        back[...] += three_pass(slope_in[:, window], w_out_in[:, window], ((1,), (1,)))
-        return carry
-
-    lax.fori_loop(0, rows, back_step, 0)
-    sigma = 1.0 / (1.0 + jnp.exp(-pre[...]))
+    squares[...] = jnp.zeros_like(squares)
+    done = 0
+    for owner in range(rows):
+        until = per_block // 2 * (owner + 1) + slack * 2 * last
+        lax.fori_loop(done, until, step, 0)
+        done = until
+
+        def shared(i, carry, owner=owner):
+            j = owner * per_block + i
+            remote(
+                spot(whole, j, core), spot(whole, j, 1 - core), share_send.at[j], share_recv.at[j], partner
+            ).wait_recv()
+            return carry
+
+        lax.fori_loop(0, per_block, shared, 0)
+        hold(velocity, owner).wait()
+        diff = whole[:, fixed(owner)] - held[:, fixed(owner)]
+        squares[...] += jnp.sum(diff * diff, axis=0, keepdims=True)
+        slope = diff * scale
+        hold(mixed, owner).start()
+        hidden = pre[...] * (1.0 / (1.0 + jnp.exp(-pre[...])))
+        local_out[:, fixed(owner)] = three_pass(hidden, slope, ((0,), (0,)))
+        over_out.ready_for(owner)
+        if owner == 0:
+            w_load.wait()
+        back[...] += three_pass(slope, w_out_in[:, fixed(owner)], ((1,), (1,)))
+        if owner > 0:
+            over_out.forward_for(owner - 1)
+
     back[...] = back[...] * sigma * (1.0 + pre[...] * (1.0 - sigma))
     sums[r, 0:1, :] = jnp.sum(fraction[...] * back[...], axis=0, keepdims=True)
-    sums[r, 1:2, :] = squared[...]
-
-    def share(k, slot):
-        return remote(sums.at[slot], sums.at[slot], sum_send.at[k], sum_recv.at[k], peers[k])
+    total = jnp.sum(squares[...], axis=1, keepdims=True)
+    sums[r, 1:2, :] = jnp.broadcast_to(total, (1, back.shape[1]))
+
+    def small(k, slot):
+        return remote(sums.at[slot], sums.at[slot], small_send.at[k], small_recv.at[k], peers[k])
 
     for k in range(rows - 1):
-        share(k, r).start()
-
-    loads[3].wait()
-    over_out.forward()
+        small(k, r).start()
+    for owner in range(rows):
+        hold(mixed, owner).wait()
     order = over_in.order()
     for place in range(rows):
         owner = order[place]
-        local_in[columns(owner), :] = three_pass(mixed_in[:, columns(owner)], back[...], ((0,), (0,)))
+        local_in[columns(owner), :] = three_pass(held[:, columns(owner)], back[...], ((0,), (0,)))
         over_in.ready(place)
+        if place == 0:
+            over_out.forward_for(rows - 1)
         if place == rows - 2:
             over_in.forward()
     for k in range(rows - 1):
-        share(k, lax.rem(r + rows - 1 - k, rows)).wait_recv()
+        small(k, lax.rem(r + rows - 1 - k, rows)).wait_recv()
     for k in range(rows - 1):
-        share(k, r).wait_send()
+        small(k, r).wait_send()
     both = sums[0]
     for k in range(1, rows):
         both = both + sums[k]
     grad_time[...] = both[0:1]
     error[...] = both[1:2]
+
+    def finish(j, carry):
+        pair(j).wait_send()
+        share(j).wait_send()
+        here = jnp.where(lax.rem(j, 2) == 0, z, last - z)
+
+        @pl.when(here < last)
+        def _():
+            hop(j, partner).wait_send()
+
+        @pl.when(here > 0)
+        def _():
+            cast(j, partner).wait_send()
+
+        return carry
+
+    lax.fori_loop(0, count, finish, 0)
     over_out.finish(grad_out)
     over_in.finish(grad_in)
 
 
-def gradients(fraction, pre, squared, local_out, slope, w_out, mixed, rows):
+def gradients(fraction, pre, part, velocity, w_out, mixed, rows, cols):
     points, hidden = pre.shape
     features = mixed.shape[1]
     block = features // rows
+    count = 32
     dma = pltpu.SemaphoreType.DMA
     vmem = functools.partial(pltpu.VMEM, dtype=jnp.float32)
     anywhere = pl.BlockSpec(memory_space=pl.ANY)
     inside = pl.BlockSpec(memory_space=pltpu.VMEM)
     boxes = 2 if rows == 4 else rows - 1
     copies = max(rows, 6)
+    scale = (points * rows) ** -0.5
 
     def result(*shape):
         return jax.ShapeDtypeStruct(shape, jnp.float32)
 
     return pl.pallas_call(
-        functools.partial(backward_kernel, rows),
+        functools.partial(backward_kernel, rows, cols // 2, count, SLACK, scale),
         out_shape=(
             result(block, hidden), result(hidden, block), result(1, hidden), result(1, hidden),
         ),
-        in_specs=[inside] * 3 + [anywhere] * 4,
+        in_specs=[inside] * 2 + [anywhere] * 4,
         out_specs=(inside,) * 4,
         scratch_shapes=[
-            vmem((hidden, features)), vmem((points, features)), vmem((hidden, features)),
-            vmem((points, features)), vmem((features, hidden)), vmem((points, hidden)),
+            vmem((points // 2, features)), vmem((points // 2, features)), vmem((points // 2, features)),
+            vmem((points, features)), vmem((hidden, features)), vmem((points, features)),
+            vmem((hidden, features)), vmem((features, hidden)), vmem((points, hidden)), vmem((1, block)),
             vmem((boxes, hidden, block)), vmem((2, hidden // 2, block)),
             vmem((boxes, block, hidden)), vmem((2, block // 2, hidden)),
             vmem((rows, 2, hidden)),
-            dma((4,)), dma((copies,)), dma((copies,)), dma((copies,)), dma((copies,)),
+        ] + [dma((count,))] * 9 + [
+            dma((rows,)), dma((1,)), dma((copies,)), dma((copies,)), dma((copies,)), dma((copies,)),
             dma((rows,)), dma((rows,)),
         ],
         compiler_params=params(4),
         name="backward",
-    )(
-        fraction[:, None], pre, jnp.broadcast_to(squared, (1, hidden)), local_out, slope, w_out, mixed
-    )
+    )(fraction[:, None], pre, part, velocity, w_out, mixed)
 
 
 def body(rows, cols, noise, images, time_index, w_in, time_gain, w_out):
@@ -752,22 +919,10 @@
         jnp.dot(mixed, w_in, precision=high, preferred_element_type=jnp.float32)
         + fraction[:, None] * time_gain[None, :]
     )
-    sigma = jax.nn.sigmoid(pre)
-    hidden = pre * sigma
+    hidden = pre * jax.nn.sigmoid(pre)
     part_out = jnp.dot(hidden, w_out, precision=high, preferred_element_type=jnp.float32)
-    out = total_over_col(part_out, cols, 3)
-    diff = out - velocity
-    squared = jnp.sum(diff * diff)
-    slope = diff / jnp.sqrt(jnp.float32(noise_count))
-    local_out = lax.dot_general(
-        hidden,
-        slope,
-        (((0,), (0,)), ((), ())),
-        precision=high,
-        preferred_element_type=jnp.float32,
-    )
     grad_in, grad_out, grad_time, squared_all = gradients(
-        fraction, pre, squared, local_out, slope, w_out, mixed, rows
+        fraction, pre, part_out, velocity, w_out, mixed, rows, cols
     )
     mse = squared_all[0, 0] / (noise_count * width)
     return (targets, row_pot, col_pot, grad_in, grad_time[0], grad_out, mse)

time: 483 us -> 444 us (0.919)
  other arithmetic: 33.4 us -> 14.4 us
  matrix products: 45.9 us -> 34 us
    pallas_call x2 -> x1, Pallas kernels: 177 us -> 88.5 us  [total_over_col(): pl.pallas_call(functools.partial(total_kernel, chips, count, SLACK), out_...]
    pallas_call x1, Pallas kernels: 85.3 us -> 172 us  [gradients(): pl.pallas_call(functools.partial(backward_kernel, rows, cols // 2, count,...]
    div x1 -> x0, other arithmetic: 14.3 us -> none  [body(): slope = diff / jnp.sqrt(jnp.float32(noise_count))]
    dot_general x1 -> x0, matrix products: 9.83 us -> none  [body(): lax.dot_general(hidden, slope, (((0,), (0,)), ((), ())), precision=high,...]
    sub x0 -> x1, other arithmetic: none -> 7.62 us  [body(): velocity = whole_targets - full_noise]
    add x1 -> x0, other arithmetic: 6.38 us -> none  [body(): (1.0 - fraction)[:, None] * full_noise + fraction[:, None] * whole_targets]
where the time goes in v3:
time: 444 us; the launch traced here: 441 us
  Pallas kernels  377 us (85%)
  matrix products  34 us (8%)
  other arithmetic  14.4 us (3%)
  local copies, waits for them, and re-layouts  12.6 us (3%)
    pallas_call x1, Pallas kernels, gradients(): pl.pallas_call(functools.partial(backward_kernel, rows, cols // 2, count,...  172 us
    pallas_call x1, Pallas kernels, total_over_col(): pl.pallas_call(functools.partial(total_kernel, chips, count, SLACK), out_...  88.5 us
    pallas_call x1, Pallas kernels, gathered(): pl.pallas_call(functools.partial(gather_kernel, rows, chips), out_shape=(...  83.2 us
    pallas_call x1, Pallas kernels, coupled(): pl.pallas_call(functools.partial(sinkhorn_kernel, rows, cols, points * ro...  33.1 us
    dot_general x1, matrix products, body(): jnp.dot(weights, full_images, precision=high, preferred_element_type=jnp....  12.6 us
    dot_general x1, matrix products, body(): lax.dot_general(full_noise, full_images, (((1,), (1,)), ((), ())), precis...  9.06 us

profile of v3, /device:TPU:0, one launch (start us, length us, event | category | flops | bytes accessed | tf_op | source)
XLA Modules:
  0.0 440.9 jit_solution(10936689899738659579)
XLA Ops:
  0.6 83.2 %gather.1 = (f32[512,3072]{1,0:T(8,128)}, f32[768,3072]{1,0:T(8,128)}) custom-call(f32[512,384]{1,0:T(8,128)} %noise.1, f32[768,768]{1,0:T(8,128)} %images.1), custom_call_target="tpu_custom_call" | custom-call | tf_op jit(solution)/shard_map/gather/pallas_call | solution.py:204
  83.8 0.0 copy-start.2
  83.8 0.0 copy-start.1
  83.8 4.5 %multiply_reduce_fusion = f32[768]{0:T(1024)S(1)} fusion(f32[768,3072]{1,0:T(8,128)} %get-tuple-element.17), kind=kLoop, calls=%fused_computation | loop fusion | flops 4717824 | bytes 9440256 | tf_op jit(solution)/shard_map/reduce_sum | solution.py:898
  88.4 0.9 copy-done.2
  89.3 0.5 multiply_reduce_fusion.1
  89.8 2.2 copy-done.1
  92.0 9.1 %subtract_multiply_fusion.scaled = f32[512,768]{1,0:T(8,128)} fusion(f32[512,3072]{1,0:T(8,128)S(1)} %copy-done.2, f32[768,3072]{1,0:T(8,128)S(1)} %copy-done.1, f32[768]{0:T(1024)S(1)} %multiply_reduce_fusion, f32[512]{0:T(512)S(1)} %multiply_reduce_fusion.1), kind=kOutput, calls=%fused_computation.3 | convolution fusion | flops 7249330176 | bytes 17306624 | tf_op jit(solution)/shard_map/dot_general | solution.py:899
  101.1 33.1 %sinkhorn.1 = (f32[512,768]{1,0:T(8,128)}, f32[1,512]{1,0:T(1,128)}, f32[1,768]{1,0:T(1,128)}) custom-call(f32[512,768]{1,0:T(8,128)} %subtract_multiply_fusion.scaled), custom_call_target="tpu_custom_call" | custom-call | tf_op jit(solution)/shard_map/sinkhorn/pallas_call | solution.py:328
  134.2 12.6 %fusion.9.part = f32[512,3072]{1,0:T(8,128)} fusion(f32[512,768]{1,0:T(8,128)} %get-tuple-element.18, f32[768,3072]{1,0:T(8,128)} %get-tuple-element.17), kind=kOutput, calls=%fused_computation.17 | convolution fusion | flops 7247757312 | bytes 17301504 | tf_op jit(solution)/shard_map/dot_general | solution.py:908
  146.7 88.5 %total2.1 = f32[512,3072]{1,0:T(8,128)} custom-call(f32[512,3072]{1,0:T(8,128)} %fusion.9.part), custom_call_target="tpu_custom_call" | custom-call | tf_op jit(solution)/shard_map/total2/pallas_call | solution.py:506
  235.3 0.0 slice-start.2
  235.3 2.1 constant_dynamic-slice_fusion
  237.4 0.0 copy-done.4
  237.4 0.6 reduce
  238.0 0.9 copy.13.fraction
  238.9 7.6 %fusion.8 = (f32[512,3072]{1,0:T(8,128)}, f32[512,3072]{1,0:T(8,128)S(1)}) fusion(f32[512,3072]{1,0:T(8,128)} %total2.1, f32[512,3072]{1,0:T(8,128)} %get-tuple-element.16, f32[512]{0:T(512)S(1)} %get-tuple-element.28, f32[512]{0:T(512)S(1)} %get-tuple-element.27), kind=kLoop, calls=%fused_computation.16 | loop fusion | flops 6291456 | bytes 25169920 | tf_op jit(solution)/shard_map/sub | solution.py:917
  246.5 0.0 slice-done.3
  246.5 0.0 copy-done.7
  246.6 0.0 slice-start.1
  246.6 5.2 %convolution_add_fusion.pre = f32[512,384]{1,0:T(8,128)S(1)} fusion(f32[512,3072]{1,0:T(8,128)S(1)} %get-tuple-element.26.mixed, f32[3072,384]{1,0:T(8,128)S(1)} %bitcast.13, f32[384]{0:T(512)S(1)} %copy-done.7, f32[512]{0:T(512)S(1)} %get-tuple-element.28), kind=kOutput, calls=%fused_computation.4 | convolution fusion | flops 3624271872 | bytes 11800064 | tf_op jit(solution)/shard_map/dot_general | solution.py:919
  251.7 0.0 slice-done
  251.7 0.0 slice-done.1
  251.8 0.0 copy-start.3
  251.8 7.2 %fusion.part = f32[512,3072]{1,0:T(8,128)} fusion(f32[384,3072]{1,0:T(8,128)S(1)} %bitcast.11, f32[512,384]{1,0:T(8,128)S(1)} %convolution_add_fusion.pre), kind=kOutput, calls=%fused_computation.5 | convolution fusion | flops 3624665088 | bytes 11796480 | tf_op jit(solution)/shard_map/dot_general | solution.py:923
  259.0 172.2 %backward.1 = (f32[768,384]{1,0:T(8,128)}, f32[384,768]{1,0:T(8,128)}, f32[1,384]{1,0:T(1,128)}, f32[1,384]{1,0:T(1,128)}) custom-call(f32[512,1]{1,0:T(8,128)} %copy.13.fraction, f32[512,384]{1,0:T(8,128)} %copy-done.3, f32[512,3072]{1,0:T(8,128)} %fusion.part, f32[512,3072]{1,0:T(8,128)} %get-tuple-element.25.velocity, f32[384,3072]{1,0:T(8,128)} %w_out.1, ...), custom_call_target="tpu_custom_call" | custom-call | tf_op jit(solution)/shard_map/backward/pallas_call | solution.py:869
  431.2 1.2 reduce.1
  432.4 1.1 slice.3
  434.2 0.0 copy-done.6
  434.2 0.6 copy.17
  434.8 2.4 copy.18
  437.2 2.4 copy.19
  (14 shorter events, 0.0 us)
Async XLA Ops:
  83.8 5.5 %copy-start.2 = (f32[512,3072]{1,0:T(8,128)S(1)}, f32[512,3072]{1,0:T(8,128)}, u32[]{:S(2)}) copy-start(f32[512,3072]{1,0:T(8,128)} %get-tuple-element.16) | copy-start | bytes 18874372
  83.8 8.2 %copy-start.1 = (f32[768,3072]{1,0:T(8,128)S(1)}, f32[768,3072]{1,0:T(8,128)}, u32[]{:S(2)}) copy-start(f32[768,3072]{1,0:T(8,128)} %get-tuple-element.17) | copy-start | bytes 28311556
  146.7 90.7 %copy-start.4 = (f32[1,768]{1,0:T(1,128)S(1)}, f32[1,768]{1,0:T(1,128)}, u32[]{:S(2)}) copy-start(f32[1,768]{1,0:T(1,128)} %get-tuple-element.20) | copy-start | bytes 9220
  146.7 91.3 %copy-start.5 = (s32[512]{0:T(512)S(1)}, s32[512]{0:T(512)}, u32[]{:S(2)}) copy-start(s32[512]{0:T(512)} %param.8) | copy-start | bytes 6148
  235.3 11.2 %slice-start.2 = ((s8[4718592]{0:T(1024)(128)(4,1)}), s8[524288]{0:T(1024)(128)(4,1)S(1)}, s32[]{:S(2)}) async-start(s8[4718592]{0:T(1024)(128)(4,1)} %bitcast.12), calls=%async_computation.2 | async-start | bytes 1048576
  238.9 7.6 %slice-start.3 = ((s8[4718592]{0:T(1024)(128)(4,1)}), s8[4194304]{0:T(1024)(128)(4,1)S(1)}, s32[]{:S(2)}) async-start(s8[4718592]{0:T(1024)(128)(4,1)} %bitcast.12), calls=%async_computation.3 | async-start | bytes 8388608
  238.9 7.6 %copy-start.7 = (f32[384]{0:T(512)S(1)}, f32[384]{0:T(512)}, u32[]{:S(2)}) copy-start(f32[384]{0:T(512)} %param.10) | copy-start | bytes 4612
  246.5 12.5 %copy-start = (f32[512,3072]{1,0:T(8,128)}, f32[512,3072]{1,0:T(8,128)S(1)}, u32[]{:S(2)}) copy-start(f32[512,3072]{1,0:T(8,128)S(1)} %get-tuple-element.26.mixed) | copy-start | bytes 18874372
  246.5 5.2 %slice-start = ((s8[4718592]{0:T(1024)(128)(4,1)}), s8[4194304]{0:T(1024)(128)(4,1)S(1)}, s32[]{:S(2)}) async-start(s8[4718592]{0:T(1024)(128)(4,1)} %bitcast.10), calls=%async_computation | async-start | bytes 8388608
  246.6 5.2 %slice-start.1 = ((s8[4718592]{0:T(1024)(128)(4,1)}), s8[524288]{0:T(1024)(128)(4,1)S(1)}, s32[]{:S(2)}) async-start(s8[4718592]{0:T(1024)(128)(4,1)} %bitcast.10), calls=%async_computation.1 | async-start | bytes 1048576
  251.8 7.2 %copy-start.3 = (f32[512,384]{1,0:T(8,128)}, f32[512,384]{1,0:T(8,128)S(1)}, u32[]{:S(2)}) copy-start(f32[512,384]{1,0:T(8,128)S(1)} %convolution_add_fusion.pre) | copy-start | bytes 2359300
  259.0 175.2 %copy-start.6 = (f32[1,512]{1,0:T(1,128)S(1)}, f32[1,512]{1,0:T(1,128)}, u32[]{:S(2)}) copy-start(f32[1,512]{1,0:T(1,128)} %get-tuple-element.19) | copy-start | bytes 6148
